TPU v7x, 256 devices: a whole 4x4x8 slice. The times are simulated.
256 devices in a mesh: chan: 16 (over z, core), rad: 16 (over y, x).
Axes of the slice: x: 4, y: 4, z: 8, core: 2. Of those that a mesh axis runs over, the one named last changes fastest.
Arguments:
- state: float32 [2048, 2, 16, 1536], P('chan', None, None, 'rad'), may hold values from -200 to 200
- coupling: float32 [64, 16, 4, 32, 32], P('chan'), may hold values from -1.1 to 1.1
- fetch_group: int32 [16, 16], replicated, may hold values from 0 to 3
- live_slots: int32 [64], P('chan'), may hold values from 1 to 16, as said below
- radius_one: float32 [16], replicated, may hold values from 1 to 6
- radius_two: float32 [1536], P('rad'), may hold values from 1 to 6
- kinetic_diag: float32 [12, 128, 128], replicated, may hold values from -2 to 5
- kinetic_link: float32 [11, 128, 128], replicated, may hold values from -0.5 to 0.5
Outputs:
- orthogonal: float32 [2048, 2, 16, 1536], P(('chan', 'rad'))
- arnoldi_coeffs: float32 [3], replicated
Inputs may be any that keep to these rules, and one draw needn't show every extreme that they name: `live_slots`: every draw has a block with all 16 slots live.
All inputs are finite; a program needn't handle non-finite values.
Results may differ from a plain program's by a relative error of at most 0.0003.
Values sent between devices are 32-bit elements; how exact they have to be, the bound alone decides.
A program may use at most 128 MiB of HBM per device.

v0:
```python
import jax
import jax.numpy as jnp
from jax import lax
from jax.sharding import PartitionSpec as P

C = 2048
R = 1536


def radial_kernel(radius_one, radius_two, orders):
    nearer = jnp.minimum(radius_one[:, None], radius_two[None, :])
    farther = jnp.maximum(radius_one[:, None], radius_two[None, :])
    powers = jnp.arange(orders).astype(radius_one.dtype)[:, None, None]
    return nearer[None] ** powers / farther[None] ** (powers + 1.0)


def kinetic(field, kinetic_diag, kinetic_link):
    elements = kinetic_diag.shape[0]
    points = kinetic_diag.shape[1]
    rows = field.reshape(-1, elements, points)
    result = jnp.einsum("rep,eqp->req", rows, kinetic_diag, precision=lax.Precision.HIGHEST)
    lower = jnp.einsum("rep,eqp->req", rows[:, :-1], kinetic_link, precision=lax.Precision.HIGHEST)
    upper = jnp.einsum("rep,epq->req", rows[:, 1:], kinetic_link, precision=lax.Precision.HIGHEST)
    result = (
        result + jnp.pad(lower, ((0, 0), (1, 0), (0, 0))) + jnp.pad(upper, ((0, 0), (0, 1), (0, 0)))
    )
    return result.reshape(field.shape)


def coupling_products(state, coupling, fetch_group, live_slots, radius_one, radius_two):
    chan_count = lax.axis_size("chan")
    my_rank = lax.axis_index("chan")
    local_channels = state.shape[0]
    planes = state.shape[1]
    band = state.shape[2]
    radial = state.shape[3]
    groups_here = coupling.shape[0]
    orders = coupling.shape[2]
    block = coupling.shape[3]
    cells = planes * band * radial
    grouped = state.reshape(groups_here, block, cells)
    outgoing = jnp.take(grouped, fetch_group[:, my_rank], axis=0)
    incoming = lax.all_to_all(outgoing, "chan", split_axis=0, concat_axis=0, tiled=True)
    incoming = incoming.reshape(chan_count * block, cells)
    slot_of = (jnp.arange(chan_count, dtype=jnp.int32) - my_rank) % chan_count
    weights = jnp.take(coupling, slot_of, axis=1)
    active = (slot_of[None, :] < live_slots[:, None]).astype(jnp.float32)
    weights = weights * active[:, :, None, None, None]
    matrices = weights.transpose(2, 0, 3, 1, 4).reshape(orders, local_channels, chan_count * block)
    kernel = radial_kernel(radius_one, radius_two, orders)
    kernel = jnp.broadcast_to(kernel[:, None], (orders, planes, band, radial)).reshape(
        orders, cells
    )
    total = jnp.zeros((local_channels, cells), jnp.float32)
    for order in range(orders):
        product = jnp.dot(
            matrices[order],
            incoming,
            precision=lax.Precision.HIGHEST,
            preferred_element_type=jnp.float32,
        )
        total = total + kernel[order] * product
    return total.reshape(state.shape)


def per_device(
    state, coupling, fetch_group, live_slots, radius_one, radius_two, kinetic_diag, kinetic_link
):
    coupled = coupling_products(state, coupling, fetch_group, live_slots, radius_one, radius_two)
    state_here, coupled_here = (
        lax.all_to_all(state, "rad", split_axis=0, concat_axis=3, tiled=True),
        lax.all_to_all(coupled, "rad", split_axis=0, concat_axis=3, tiled=True),
    )
    applied = kinetic(state_here, kinetic_diag, kinetic_link) + coupled_here
    wave_re = applied[:, 1]
    wave_im = -applied[:, 0]
    state_re = state_here[:, 0]
    state_im = state_here[:, 1]
    total_count = 2.0 * C * state.shape[2] * R
    cross_re = jnp.sum(state_re * wave_re + state_im * wave_im)
    cross_im = jnp.sum(state_re * wave_im - state_im * wave_re)
    self_sq = jnp.sum(state_here * state_here)
    cross_re, cross_im, self_sq = lax.psum((cross_re, cross_im, self_sq), ("chan", "rad"))
    proj_re = cross_re / self_sq
    proj_im = cross_im / self_sq
    orth_re = wave_re - (proj_re * state_re - proj_im * state_im)
    orth_im = wave_im - (proj_re * state_im + proj_im * state_re)
    square_mean = (
        lax.psum(jnp.sum(orth_re * orth_re + orth_im * orth_im), ("chan", "rad")) / total_count
    )
    rms = jnp.sqrt(square_mean + 1e-06)
    orthogonal = jnp.stack([orth_re, orth_im], axis=1)
    return (orthogonal, jnp.stack([proj_re, proj_im, rms]))


def solution(mesh):
    placed = (
        P("chan", None, None, "rad"),
        P("chan", None, None, None, None),
        P(),
        P("chan"),
        P(),
        P("rad"),
        P(),
        P(),
    )
    return jax.shard_map(
        per_device,
        mesh=mesh,
        in_specs=placed,
        out_specs=(P(("chan", "rad"), None, None, None), P()),
        check_vma=False,
    )
```

profile of v0, /device:TPU:1, one launch (start us, length us, event | category | flops | bytes accessed | tf_op | source)
XLA Modules:
  0.0 410.5 jit_solution(6286049403578286027)
XLA Ops:
  2.5 3.0 copy.55
  5.5 2.5 reshape.226
  8.0 3.6 gather_fusion.1
  11.7 6.5 %broadcast_select_fusion = f32[16,32,3072]{2,1,0:T(8,128)} fusion(f32[16,32,3072]{2,1,0:T(8,128)} %gather_fusion.1, pred[16]{0:T(512)(128)(4,1)S(1)} %and_reduce_fusion), kind=kLoop, calls=%fused_computation.11 | loop fusion | flops 1572864 | bytes 12582928 | tf_op jit(solution)/shard_map/jit(_take)/select_n | solution.py:42
  18.1 10.0 %all-to-all-start.1 = ((f32[16,32,3072]{2,1,0:T(8,128)}), f32[16,32,3072]{2,1,0:T(8,128)}, u32[]{:S(2)}, u32[]{:S(2)}) async-start(f32[16,32,3072]{2,1,0:T(8,128)} %broadcast_select_fusion), calls=%async_computation.1 | async-start | bytes 12582912 | tf_op jit(solution)/shard_map/all_to_all | solution.py:43
  28.2 5.0 %gather_fusion = f32[16,4,4,32,32]{4,3,2,1,0:T(8,128)} fusion(f32[4,16,4,32,32]{4,3,2,1,0:T(8,128)} %param.9, s32[1024]{0:T(1024)S(1)} %pad_clamp_fusion.1), kind=kCustom, calls=%fused_computation | custom fusion | bytes 2097216 | tf_op jit(solution)/shard_map/jit(_take)/gather | solution.py:46
  33.3 2.5 fusion
  35.9 1.9 fusion.24
  46.3 120.3 %all-to-all-done.1 = f32[16,32,3072]{2,1,0:T(8,128)} async-done(((f32[16,32,3072]{2,1,0:T(8,128)}), f32[16,32,3072]{2,1,0:T(8,128)}, u32[]{:S(2)}, u32[]{:S(2)}) %all-to-all-start.1) | async-done | bytes 6291488 | tf_op jit(solution)/shard_map/all_to_all | solution.py:43
  166.6 6.8 %all-to-all-start = ((f32[128,2,16,96]{3,2,1,0:T(8,128)}), f32[128,2,16,96]{3,2,1,0:T(8,128)S(1)}, u32[]{:S(2)}, u32[]{:S(2)}) async-start(f32[128,2,16,96]{3,2,1,0:T(8,128)} %copy.55), calls=%async_computation | async-start | bytes 4194304 | tf_op jit(solution)/shard_map/all_to_all | solution.py:71
  173.4 5.6 %convolution_multiply_fusion.3 = f32[128,3072]{1,0:T(8,128)S(1)} fusion(f32[128,512]{1,0:T(8,128)S(1)} %squeeze.23, f32[512,3072]{1,0:T(8,128)} %bitcast.8, f32[3072]{0:T(1024)S(1)} %broadcast_in_dim.51), kind=kOutput, calls=%fused_computation.10 | convolution fusion | flops 2416312320 | bytes 8138752 | tf_op jit(solution)/shard_map/dot_general | solution.py:56
  179.0 5.6 %fusion.3 = f32[128,3072]{1,0:T(8,128)S(1)} fusion(f32[128,3072]{1,0:T(8,128)S(1)} %convolution_multiply_fusion.3, f32[128,512]{1,0:T(8,128)S(1)} %squeeze.24, f32[512,3072]{1,0:T(8,128)} %bitcast.8, f32[3072]{0:T(1024)S(1)} %broadcast_in_dim.57), kind=kOutput, calls=%fused_computation.9 | convolution fusion | flops 2416705536 | bytes 9711616 | tf_op jit(solution)/shard_map/dot_general | solution.py:56
  184.6 5.6 %fusion.2 = f32[128,3072]{1,0:T(8,128)S(1)} fusion(f32[128,3072]{1,0:T(8,128)S(1)} %fusion.3, f32[128,512]{1,0:T(8,128)S(1)} %copy-done.6, f32[512,3072]{1,0:T(8,128)} %bitcast.8, f32[3072]{0:T(1024)S(1)} %broadcast_in_dim.59), kind=kOutput, calls=%fused_computation.7 | convolution fusion | flops 2416705536 | bytes 9711616 | tf_op jit(solution)/shard_map/dot_general | solution.py:56
  190.2 7.3 %fusion.1 = f32[128,3072]{1,0:T(8,128)} fusion(f32[128,3072]{1,0:T(8,128)S(1)} %fusion.2, f32[128,512]{1,0:T(8,128)S(1)} %copy-done.7, f32[512,3072]{1,0:T(8,128)} %bitcast.8, f32[3072]{0:T(1024)S(1)} %broadcast_in_dim.61), kind=kOutput, calls=%fused_computation.5 | convolution fusion | flops 2416705536 | bytes 9711616 | tf_op jit(solution)/shard_map/dot_general | solution.py:56
  197.6 3.0 copy.67
  200.6 3.0 copy.68
  204.9 6.7 %all-to-all-start.2 = ((f32[128,2,16,96]{3,2,1,0:T(8,128)}), f32[128,2,16,96]{3,2,1,0:T(8,128)}, u32[]{:S(2)}, u32[]{:S(2)}) async-start(f32[128,2,16,96]{3,2,1,0:T(8,128)} %copy.68), calls=%async_computation.2 | async-start | bytes 4194304 | tf_op jit(solution)/shard_map/all_to_all | solution.py:72
  211.7 2.8 copy.56
  217.5 2.2 all_to_all.37
  219.7 2.2 copy.57
  224.8 2.8 fusion.4
  227.6 2.9 copy.61
  230.5 2.6 reshape.225
  233.1 2.7 multiply_reduce_fusion
  235.8 4.0 all-to-all-done.2
  239.8 4.1 %copy.69 = f32[8,2,16,16,96]{4,3,2,1,0:T(8,128)} copy(f32[8,2,16,16,96]{4,2,1,0,3:T(8,128)} %bitcast.14) | data formatting | bytes 3145728 | tf_op jit(solution)/shard_map/all_to_all | solution.py:72
  244.0 3.1 all_to_all.36
  247.0 2.1 add.110
  250.3 77.7 %all-reduce.2 = (f32[]{:T(128)}, f32[]{:T(128)}, f32[]{:T(128)}) all-reduce(f32[]{:T(128)} %get-tuple-element.3, f32[]{:T(128)} %multiply_reduce_fusion, f32[]{:T(128)} %get-tuple-element.2), channel_id=1, replica_groups=mesh['chan'=16,'rad'=16] {'chan','rad'}, use_global_device_ids=true, to_apply=%region_5.6 | all-reduce | flops 3 | bytes 24 | tf_op jit(solution)/shard_map/psum | solution.py:83
  330.5 2.4 fusion.13
  334.2 72.6 %psum.31 = f32[]{:T(128)} all-reduce(f32[]{:T(128)} %fusion.13), channel_id=1, replica_groups=mesh['chan'=16,'rad'=16] {'chan','rad'}, use_global_device_ids=true, to_apply=%region_7.8 | all-reduce | flops 1 | bytes 8 | tf_op jit(solution)/shard_map/psum | solution.py:89
  407.5 2.4 pad_maximum_fusion
  (58 shorter events, 20.7 us)
Async XLA Ops:
  0.6 224.2 %copy-start = (f32[12,128,128]{2,1,0:T(8,128)S(1)}, f32[12,128,128]{2,1,0:T(8,128)}, u32[]{:S(2)}) copy-start(f32[12,128,128]{2,1,0:T(8,128)} %param.14) | copy-start | bytes 2359300
  18.1 148.5 %all-to-all-start.1 = ((f32[16,32,3072]{2,1,0:T(8,128)}), f32[16,32,3072]{2,1,0:T(8,128)}, u32[]{:S(2)}, u32[]{:S(2)}) async-start(f32[16,32,3072]{2,1,0:T(8,128)} %broadcast_select_fusion), calls=%async_computation.1 | async-start | bytes 12582912 | tf_op jit(solution)/shard_map/all_to_all | solution.py:43
  28.2 5.0 %copy-start.8 = (s32[4]{0:T(128)S(1)}, s32[4]{0:T(128)}, u32[]{:S(2)}) copy-start(s32[4]{0:T(128)} %param.11) | copy-start | bytes 52
  37.8 1.1 copy-start.9
  37.8 1.1 copy-start.10
  166.6 37.0 %all-to-all-start = ((f32[128,2,16,96]{3,2,1,0:T(8,128)}), f32[128,2,16,96]{3,2,1,0:T(8,128)S(1)}, u32[]{:S(2)}, u32[]{:S(2)}) async-start(f32[128,2,16,96]{3,2,1,0:T(8,128)} %copy.55), calls=%async_computation | async-start | bytes 4194304 | tf_op jit(solution)/shard_map/all_to_all | solution.py:71
  179.0 5.6 %copy-start.6 = (f32[128,512]{1,0:T(8,128)S(1)}, f32[128,512]{1,0:T(8,128)}, u32[]{:S(2)}) copy-start(f32[128,512]{1,0:T(8,128)} %squeeze.25) | copy-start | bytes 786436
  184.6 5.6 %copy-start.7 = (f32[128,512]{1,0:T(8,128)S(1)}, f32[128,512]{1,0:T(8,128)}, u32[]{:S(2)}) copy-start(f32[128,512]{1,0:T(8,128)} %squeeze.26) | copy-start | bytes 786436
  203.6 1.3 copy-start.4
  204.9 34.9 %all-to-all-start.2 = ((f32[128,2,16,96]{3,2,1,0:T(8,128)}), f32[128,2,16,96]{3,2,1,0:T(8,128)}, u32[]{:S(2)}, u32[]{:S(2)}) async-start(f32[128,2,16,96]{3,2,1,0:T(8,128)} %copy.68), calls=%async_computation.2 | async-start | bytes 4194304 | tf_op jit(solution)/shard_map/all_to_all | solution.py:72
  214.4 1.4 copy-start.3
  219.7 2.2 copy-start.5
  249.1 1.1 copy-start.1
  330.5 2.4 copy-start.2
where the time goes:
time: 412 us; the launch traced here: 410 us
  blocking collectives  150 us (36%)
  waiting for transfers between devices  124 us (30%)
  local copies, waits for them, and re-layouts  54.6 us (13%)
  matrix products  29.7 us (7%)
  other arithmetic  23.9 us (6%)
  starting transfers between devices  23.5 us (6%)
  between operations  4.18 us (1%)
    all_to_all x1, waiting for transfers between devices, coupling_products(): lax.all_to_all(outgoing, 'chan', split_axis=0, concat_axis=0, tiled=True)  120 us
    psum x1, blocking collectives, per_device(): lax.psum((cross_re, cross_im, self_sq), ('chan', 'rad'))  77.7 us
    psum x1, blocking collectives, per_device(): lax.psum(jnp.sum(orth_re * orth_re + orth_im * orth_im), ('chan', 'rad'))  72.6 us
    dot_general x4, matrix products, coupling_products(): jnp.dot(matrices[order], incoming, precision=lax.Precision.HIGHEST, prefe...  24.1 us
    all_to_all x1, starting transfers between devices, coupling_products(): lax.all_to_all(outgoing, 'chan', split_axis=0, concat_axis=0, tiled=True)  9.98 us
  transfers between devices with their start and end apart: 3, of which 2 were waited for; matrix products, arithmetic and copies ran while one was open for 17% of the time, Pallas kernels for 0%

commit v1 on v0

v1 whole, which is shorter than its diff:
```python
import functools

import jax
import jax.numpy as jnp
from jax import lax
from jax.experimental import pallas as pl
from jax.experimental.pallas import tpu as pltpu
from jax.sharding import PartitionSpec as P

MESH = pl.DeviceIdType.MESH
F32 = jnp.float32
BF16 = jnp.bfloat16

C = 2048
R = 1536
B = 16
DEV = 16
Q = 4
CELLS = 768
GS = 32
T = 12
GROUPS = 1 + T // 2
LANES = 128
PTS = 96


def split(x):
    high = x.astype(BF16)
    return high, (x - high.astype(F32)).astype(BF16)


def pack4(a, b, c, d):
    return (
        jnp.concatenate([a, d[:, 0:32]], axis=1),
        jnp.concatenate([b, d[:, 32:64]], axis=1),
        jnp.concatenate([c, d[:, 64:96]], axis=1),
    )


def unpack4(t0, t1, t2):
    last = jnp.concatenate([t0[:, 96:128], t1[:, 96:128], t2[:, 96:128]], axis=1)
    return t0[:, 0:96], t1[:, 0:96], t2[:, 0:96], last


def kernel(
    state_ref,
    coup_ref,
    fetch_ref,
    live_ref,
    r1_ref,
    r2_ref,
    diag_ref,
    link_ref,
    out_ref,
    coef_ref,
    xp,
    sibx,
    pool,
    stage,
    wh,
    wl,
    kern,
    acc,
    cpl,
    srecv,
    crecv,
    snat,
    app,
    rows_of,
    part,
    gath,
    ring_send,
    ring_recv,
    sib_send,
    sib_recv,
    sx_send,
    sx_recv,
    st_send,
    st_recv,
    cp_send,
    cp_recv,
    sc_send,
    sc_recv,
):
    me = lax.axis_index("chan")
    rad = lax.axis_index("rad")
    core = lax.rem(me, 2)
    sib = me + 1 - 2 * core
    up = (lax.rem(me + 2, DEV), rad)
    down = (lax.rem(me + DEV - 2, DEV), rad)
    sibling = (sib, rad)

    def chan_peer(k):
        return (lax.rem(me + k, DEV), rad)

    def rad_peer(k):
        return (me, lax.rem(rad + k, DEV))

    barrier = pltpu.get_barrier_semaphore()
    for k in range(1, DEV):
        pl.semaphore_signal(barrier, inc=1, device_id=chan_peer(k), device_id_type=MESH)
        pl.semaphore_signal(barrier, inc=1, device_id=rad_peer(k), device_id_type=MESH)

    for q in range(Q):
        for plane in range(2):
            rows = [
                state_ref[pl.ds(plane * B + 4 * q + i, 128, stride=2 * B), :]
                for i in range(4)
            ]
            for i, tile in enumerate(pack4(*rows)):
                at = (plane * 3 + i) * LANES
                xp[q, :, at : at + LANES] = tile

    pl.semaphore_wait(barrier, 2 * (DEV - 1))

    def slot(t, side, way):
        return (t * 4 + side * 2 + way) * GS

    def ring_copy(q, t, way, src):
        return pltpu.make_async_remote_copy(
            src_ref=src,
            dst_ref=pool.at[q, pl.ds(slot(t, 0, way), GS), :],
            send_sem=ring_send.at[way, q, t],
            recv_sem=ring_recv.at[way, q, t],
            device_id=(up, down)[way],
            device_id_type=MESH,
        )

    def ring_src(q, t, way):
        if t < 4:
            return xp.at[q, pl.ds(GS * t, GS), :]
        if t < 8:
            return pool.at[q, pl.ds(slot(t - 4, 0, way), GS), :]
        if t < 11:
            return stage.at[q, way * 3 + t - 8]
        return pool.at[q, pl.ds(slot(10, 0, way), GS), :]

    def fetched(dest, source):
        return fetch_ref[dest, source]

    def wrap(x):
        return lax.rem(x + 2 * DEV, DEV)

    picks = []
    for way in range(2):
        sign = 1 if way == 0 else -1
        source = wrap(me - 4 * sign)
        near = wrap(me - core + 2 * sign)
        far = wrap(me - core + 4 * sign)
        far_core = core if way == 0 else 1 - core
        picks.append(
            [
                fetched(near, source),
                fetched(near + 1, source),
                fetched(far + far_core, source),
            ]
        )

    def ring_start(q, t):
        for way in range(2):
            if 8 <= t < 11:
                pick = picks[way][t - 8]
                chosen = pool[q, pl.ds(slot(4, 0, way), GS), :]
                for h in range(1, 4):
                    chosen = jnp.where(
                        pick == h, pool[q, pl.ds(slot(4 + h, 0, way), GS), :], chosen
                    )
                stage[q, way * 3 + t - 8] = chosen
            ring_copy(q, t, way, ring_src(q, t, way)).start()

    def sib_copy(q, t):
        return pltpu.make_async_remote_copy(
            src_ref=pool.at[q, pl.ds(slot(t, 0, 0), 2 * GS), :],
            dst_ref=pool.at[q, pl.ds(slot(t, 1, 0), 2 * GS), :],
            send_sem=sib_send.at[q, t],
            recv_sem=sib_recv.at[q, t],
            device_id=sibling,
            device_id_type=MESH,
        )

    def arrived(q, t):
        for way in range(2):
            ring_copy(q, t, way, ring_src(q, t, way)).wait_recv()
        sib_copy(q, t).start()

    def sib_arrived(q, t):
        sib_copy(q, t).wait_recv()

    sibx_copy = pltpu.make_async_remote_copy(
        src_ref=xp,
        dst_ref=sibx,
        send_sem=sx_send.at[0],
        recv_sem=sx_recv.at[0],
        device_id=sibling,
        device_id_type=MESH,
    )

    def state_copy(k):
        return pltpu.make_async_remote_copy(
            src_ref=xp.at[:, pl.ds(8 * lax.rem(rad + k, DEV), 8), :],
            dst_ref=srecv.at[rad],
            send_sem=st_send.at[k],
            recv_sem=st_recv.at[k],
            device_id=rad_peer(k),
            device_id_type=MESH,
        )

    def coupled_copy(q, k):
        return pltpu.make_async_remote_copy(
            src_ref=cpl.at[q, pl.ds(8 * lax.rem(rad + k, DEV), 8), :],
            dst_ref=crecv.at[q, rad],
            send_sem=cp_send.at[q, k],
            recv_sem=cp_recv.at[q, k],
            device_id=rad_peer(k),
            device_id_type=MESH,
        )

    ring_start(0, 0)
    ring_start(0, 1)
    sibx_copy.start()
    for k in range(1, DEV):
        state_copy(k).start()
    ring_start(0, 2)
    ring_start(0, 3)
    srecv[rad] = xp[:, pl.ds(pl.multiple_of(8 * rad, 8), 8), :]

    row = jnp.broadcast_to(r2_ref[0:1, :], (8, PTS))
    tails = pack4(row, row, row, row)
    lane = lax.broadcasted_iota(jnp.int32, (8, LANES), 1)
    for q in range(Q):
        for i in range(3):
            one = jnp.where(lane < PTS, r1_ref[4 * q + i], r1_ref[4 * q + 3])
            nearer = jnp.minimum(one, tails[i])
            farther = jnp.maximum(one, tails[i])
            top = jnp.ones_like(nearer)
            bottom = farther
            for order in range(4):
                value = top / bottom
                for plane in range(2):
                    at = (plane * 3 + i) * LANES
                    kern[q, order, :, at : at + LANES] = value
                top = top * nearer
                bottom = bottom * farther

    def put_weight(group, place, k, take):
        for g in range(4):
            on = jnp.where(live_ref[g] > k, take, 0.0)
            for order in range(4):
                start = ((g * 16 + k) * 4 + order) * GS
                block = coup_ref[pl.ds(pl.multiple_of(start, GS), GS), :] * on
                high, low = split(block)
                rows = slice(order * 128 + g * GS, order * 128 + g * GS + GS)
                cols = slice(place * GS, place * GS + GS)
                wh[group, rows, cols] = high
                wl[group, rows, cols] = low

    def one_if(condition):
        return jnp.where(condition, 1.0, 0.0)

    def build(group):
        if group == 0:
            for h in range(4):
                put_weight(0, h, 0, one_if(fetched(me, me) == h))
                put_weight(
                    0, 4 + h, wrap(sib - me), one_if(fetched(me, sib) == h)
                )
            return
        for t in (2 * group - 2, 2 * group - 1):
            dist = 1 if t < 4 else 2 if t < 8 else 3 if t < 11 else 4
            for side in range(2):
                for way in range(2):
                    home = me if side == 0 else sib
                    source = wrap(home - 2 * dist if way == 0 else home + 2 * dist)
                    if t < 8:
                        take = one_if(fetched(me, source) == t % 4)
                    elif t < 10:
                        take = one_if(core == t - 8)
                    elif t == 10:
                        take = 0.0
                    else:
                        take = float(side == way)
                    place = (t % 2) * 4 + side * 2 + way
                    put_weight(group, place, wrap(source - me), take)

    def multiply(q, group, read):
        @pl.loop(0, 3)
        def _(j):
            at = pl.multiple_of(j * 256, 256)
            xh, xl = split(read(at))
            dot = functools.partial(jnp.dot, preferred_element_type=F32)
            total = dot(wh[group], xh) + dot(wl[group], xh) + dot(wh[group], xl)
            if group == 0:
                acc[:, pl.ds(at, 256)] = total
            else:
                acc[:, pl.ds(at, 256)] += total

    def compute(q, group):
        if group == 0:
            multiply(
                q,
                0,
                lambda at: jnp.concatenate(
                    [xp[q, :, pl.ds(at, 256)], sibx[q, :, pl.ds(at, 256)]], axis=0
                ),
            )
        else:
            multiply(
                q,
                group,
                lambda at: pool[q, pl.ds(256 * (group - 1), 256), pl.ds(at, 256)],
            )

    def finish_chunk(q):
        for tile in range(6):
            cols = slice(tile * LANES, tile * LANES + LANES)
            total = jnp.zeros((128, LANES), F32)
            for order in range(4):
                factor = jnp.broadcast_to(kern[q, order, 0:1, cols], (128, LANES))
                total = total + acc[order * 128 : order * 128 + 128, cols] * factor
            cpl[q, :, cols] = total
        for k in range(1, DEV):
            coupled_copy(q, k).start()
        crecv[q, rad] = cpl[q, pl.ds(pl.multiple_of(8 * rad, 8), 8), :]

    def natural(piece):
        out = []
        for plane in range(2):
            cols = [slice((plane * 3 + i) * LANES, (plane * 3 + i + 1) * LANES) for i in range(3)]
            parts = [unpack4(*(piece(s, c) for c in cols)) for s in range(4)]
            for i in range(4):
                out.append(jnp.concatenate([p[i] for p in parts], axis=1))
        return out

    def kinetic_all():
        for k in range(1, DEV):
            state_copy(k).wait_recv()
        for q in range(Q):
            for quad in range(4):
                for i, value in enumerate(
                    natural(lambda s, c: srecv[4 * quad + s, q, :, c])
                ):
                    rows = slice(q * 64 + i * 8, q * 64 + i * 8 + 8)
                    snat[rows, 384 * quad : 384 * quad + 384] = value
        high = functools.partial(
            lax.dot_general, precision=lax.Precision.HIGHEST, preferred_element_type=F32
        )
        same = (((1,), (1,)), ((), ()))
        flip = (((1,), (0,)), ((), ()))
        for e in range(12):
            cols = [slice(128 * x, 128 * x + 128) for x in (e - 1, e, e + 1)]
            value = high(snat[:, cols[1]], diag_ref[e], same)
            if e > 0:
                value = value + high(snat[:, cols[0]], link_ref[e - 1], same)
            if e < 11:
                value = value + high(snat[:, cols[2]], link_ref[e], flip)
            app[:, cols[1]] = value

    def receive_coupled(q):
        for k in range(1, DEV):
            coupled_copy(q, k).wait_recv()
        for quad in range(4):
            for i, value in enumerate(
                natural(lambda s, c: crecv[q, 4 * quad + s, :, c])
            ):
                rows = pl.ds(pl.multiple_of(q * 64 + i * 8, 8), 8)
                cols = slice(384 * quad, 384 * quad + 384)
                app[rows, cols] += value

    def tail(q):
        arrived(q, 11)
        sib_arrived(q, 10)
        sib_arrived(q, 11)
        compute(q, 6)
        finish_chunk(q)

    build(0)
    sibx_copy.wait_recv()

    @pl.loop(0, Q)
    def _(q):
        nxt = q + 1
        more = q < Q - 1
        arrived(q, 0)
        ring_start(q, 4)
        arrived(q, 1)
        ring_start(q, 5)

        @pl.when(q > 0)
        def _():
            tail(q - 1)

        arrived(q, 2)
        ring_start(q, 6)
        arrived(q, 3)
        ring_start(q, 7)

        @pl.when(q == 0)
        def _():
            for group in range(1, 4):
                build(group)

        compute(q, 0)

        @pl.when(more)
        def _():
            ring_start(nxt, 0)
            ring_start(nxt, 1)

        sib_arrived(q, 0)
        sib_arrived(q, 1)
        compute(q, 1)
        for t in range(4, 8):
            arrived(q, t)
        for t in range(8, 11):
            ring_start(q, t)

        @pl.when(more)
        def _():
            ring_start(nxt, 2)
            ring_start(nxt, 3)

        @pl.when(q == 0)
        def _():
            for group in range(4, GROUPS):
                build(group)

        sib_arrived(q, 2)
        sib_arrived(q, 3)
        compute(q, 2)
        for t in range(8, 11):
            arrived(q, t)
        ring_start(q, 11)
        for t in range(4, 10):
            sib_arrived(q, t)
        for group in range(3, 6):
            compute(q, group)

        @pl.when(q == 0)
        def _():
            kinetic_all()

        @pl.when(q > 0)
        def _():
            receive_coupled(q - 1)

    tail(Q - 1)
    receive_coupled(Q - 1)

    def parts(q):
        re = pl.ds(q * 64, 32)
        im = pl.ds(q * 64 + 32, 32)
        return snat[re, :], snat[im, :], app[re, :], app[im, :]

    def fold(x):
        return jnp.sum(x, axis=0, keepdims=True)

    sums = [jnp.zeros((1, R), F32) for _ in range(3)]
    for q in range(Q):
        sre, sim, are, aim = parts(q)
        sums[0] += fold(sre * aim - sim * are)
        sums[1] -= fold(sre * are + sim * aim)
        sums[2] += fold(sre * sre + sim * sim)
    cross_re, cross_im, self_sq = (jnp.sum(x, axis=1, keepdims=True) for x in sums)

    def ratio(x, y):
        return jnp.where(y > 0.0, x / jnp.where(y > 0.0, y, 1.0), 0.0)

    own_re, own_im = ratio(cross_re, self_sq), ratio(cross_im, self_sq)
    left = jnp.zeros((1, R), F32)
    for q in range(Q):
        sre, sim, are, aim = parts(q)
        ore = aim - (own_re * sre - own_im * sim)
        oim = -are - (own_re * sim + own_im * sre)
        left += fold(ore * ore + oim * oim)
    left = jnp.sum(left, axis=1, keepdims=True)
    for i, value in enumerate((cross_re, cross_im, self_sq, left)):
        part[0, i : i + 1, :] = jnp.broadcast_to(value, (1, LANES))

    def scalar_copy(stage_, k):
        return pltpu.make_async_remote_copy(
            src_ref=part.at[stage_],
            dst_ref=gath.at[stage_, (me, rad)[stage_]],
            send_sem=sc_send.at[stage_, k],
            recv_sem=sc_recv.at[stage_, k],
            device_id=(chan_peer, rad_peer)[stage_](k),
            device_id_type=MESH,
        )

    def merge(stage_):
        for k in range(1, DEV):
            scalar_copy(stage_, k).start()
        gath[stage_, (me, rad)[stage_]] = part[stage_]
        for k in range(1, DEV):
            scalar_copy(stage_, k).wait_recv()
        rows = [[gath[stage_, j, i : i + 1, :] for j in range(DEV)] for i in range(4)]
        add = lambda xs: functools.reduce(lambda x, y: x + y, xs)
        cre, cim, sq = add(rows[0]), add(rows[1]), add(rows[2])
        pre, pim = ratio(cre, sq), ratio(cim, sq)
        rest = add(rows[3])
        for j in range(DEV):
            dre = pre - ratio(rows[0][j], rows[2][j])
            dim = pim - ratio(rows[1][j], rows[2][j])
            rest = rest + (dre * dre + dim * dim) * rows[2][j]
        return cre, cim, sq, rest, pre, pim

    merged = merge(0)
    for i in range(4):
        part[1, i : i + 1, :] = merged[i]
    _, _, _, rest, pre, pim = merge(1)
    rms = jnp.sqrt(rest / (2.0 * C * B * R) + 1e-06)
    coef_ref[0:1, :] = pre
    coef_ref[1:2, :] = pim
    coef_ref[2:3, :] = rms
    pre1, pim1 = pre[:, 0:1], pim[:, 0:1]
    for q in range(Q):
        for i in range(4):
            re = slice(q * 64 + i * 8, q * 64 + i * 8 + 8)
            im = slice(q * 64 + 32 + i * 8, q * 64 + 32 + i * 8 + 8)
            sre, sim, are, aim = snat[re, :], snat[im, :], app[re, :], app[im, :]
            ore = aim - (pre1 * sre - pim1 * sim)
            oim = -are - (pre1 * sim + pim1 * sre)
            for tile in range(R // LANES):
                cols = slice(tile * LANES, tile * LANES + LANES)
                rows = tile * 256 + 4 * q + i
                rows_of[pl.ds(rows, 8, stride=2 * B), :] = ore[:, cols]
                rows_of[pl.ds(rows + B, 8, stride=2 * B), :] = oim[:, cols]
    for tile in range(R // LANES):
        out_ref[:, tile * LANES : tile * LANES + LANES] = rows_of[tile * 256 : tile * 256 + 256, :]

    sibx_copy.wait_send()
    for k in range(1, DEV):
        state_copy(k).wait_send()
        scalar_copy(0, k).wait_send()
        scalar_copy(1, k).wait_send()

    @pl.loop(0, Q)
    def _(q):
        for t in range(T):
            for way in range(2):
                ring_copy(q, t, way, ring_src(q, t, way)).wait_send()
            sib_copy(q, t).wait_send()
        for k in range(1, DEV):
            coupled_copy(q, k).wait_send()


def per_device(
    state, coupling, fetch_group, live_slots, radius_one, radius_two, kinetic_diag, kinetic_link
):
    vmem = pl.BlockSpec(memory_space=pltpu.VMEM)
    smem = pl.BlockSpec(memory_space=pltpu.SMEM)
    dma = pltpu.SemaphoreType.DMA
    out, coef = pl.pallas_call(
        kernel,
        out_shape=(
            jax.ShapeDtypeStruct((8 * 2 * B, R), F32),
            jax.ShapeDtypeStruct((8, LANES), F32),
        ),
        in_specs=[vmem, vmem, smem, smem, smem, vmem, vmem, vmem],
        out_specs=(vmem, vmem),
        scratch_shapes=[
            pltpu.VMEM((Q, 128, CELLS), F32),
            pltpu.VMEM((Q, 128, CELLS), F32),
            pltpu.VMEM((Q, T * 4 * GS, CELLS), F32),
            pltpu.VMEM((Q, 6, GS, CELLS), F32),
            pltpu.VMEM((GROUPS, 512, 256), BF16),
            pltpu.VMEM((GROUPS, 512, 256), BF16),
            pltpu.VMEM((Q, 4, 8, CELLS), F32),
            pltpu.VMEM((512, CELLS), F32),
            pltpu.VMEM((Q, 128, CELLS), F32),
            pltpu.VMEM((DEV, Q, 8, CELLS), F32),
            pltpu.VMEM((Q, DEV, 8, CELLS), F32),
            pltpu.VMEM((256, R), F32),
            pltpu.VMEM((256, R), F32),
            pltpu.VMEM((R // LANES * 256, LANES), F32),
            pltpu.VMEM((2, 8, LANES), F32),
            pltpu.VMEM((2, DEV, 8, LANES), F32),
            dma((2, Q, T)),
            dma((2, Q, T)),
            dma((Q, T)),
            dma((Q, T)),
            dma((1,)),
            dma((1,)),
            dma((DEV,)),
            dma((DEV,)),
            dma((Q, DEV)),
            dma((Q, DEV)),
            dma((2, DEV)),
            dma((2, DEV)),
        ],
        compiler_params=pltpu.CompilerParams(
            collective_id=0, has_side_effects=True, vmem_limit_bytes=61 << 20
        ),
    )(
        state.reshape(128 * 2 * B, PTS),
        coupling.reshape(4 * 16 * 4 * GS, GS),
        fetch_group,
        live_slots,
        radius_one,
        radius_two.reshape(1, PTS),
        kinetic_diag,
        kinetic_link,
    )
    return out.reshape(8, 2, B, R), coef[0:3, 0]


def solution(mesh):
    placed = (
        P("chan", None, None, "rad"),
        P("chan", None, None, None, None),
        P(),
        P("chan"),
        P(),
        P("rad"),
        P(),
        P(),
    )
    return jax.shard_map(
        per_device,
        mesh=mesh,
        in_specs=placed,
        out_specs=(P(("chan", "rad"), None, None, None), P()),
        check_vma=False,
    )
```

time: 412 us -> 164 us (0.40)
  Pallas kernels: 0 us -> 156 us
  blocking collectives: 150 us -> 0 us
  waiting for transfers between devices: 124 us -> 0 us
  local copies, waits for them, and re-layouts: 54.6 us -> 7 us
  matrix products: 29.7 us -> 0 us
  other arithmetic: 23.9 us -> 0 us
  starting transfers between devices: 23.5 us -> 0 us
    pallas_call x0 -> x1, Pallas kernels: none -> 156 us  [per_device(): pl.pallas_call(kernel, out_shape=(jax.ShapeDtypeStruct((8 * 2 * B, R), F3...]
    psum x2 -> x0, blocking collectives: 150 us -> none  [the longest x1 77.7 us: per_device(): lax.psum((cross_re, cross_im, self_sq), ('chan', 'rad'))]
    all_to_all x3 -> x0, waiting for transfers between devices: 124 us -> none  [the longest x1 120 us: coupling_products(): lax.all_to_all(outgoing, 'chan', split_axis=0, concat_axis=0, tiled=True)]
    dot_general x7 -> x0, matrix products: 29.7 us -> none  [the longest x4 24.1 us: coupling_products(): jnp.dot(matrices[order], incoming, precision=lax.Precision.HIGHEST, prefe...]
    all_to_all x3 -> x0, starting transfers between devices: 23.5 us -> none  [the longest x1 9.98 us: coupling_products(): lax.all_to_all(outgoing, 'chan', split_axis=0, concat_axis=0, tiled=True)]
    all_to_all x4 -> x0, local copies, waits for them, and re-layouts: 12.2 us -> none  [the longest x2 7.2 us: per_device(): lax.all_to_all(coupled, 'rad', split_axis=0, concat_axis=3, tiled=True)]
    reshape x5 -> x0, local copies, waits for them, and re-layouts: 11.9 us -> none  [the longest x2 3.81 us: kinetic(): rows = field.reshape(-1, elements, points)]
    gather x2 -> x0, local copies, waits for them, and re-layouts: 8.57 us -> none  [the longest x1 4.97 us: coupling_products(): weights = jnp.take(coupling, slot_of, axis=1)]
  transfers between devices with their start and end apart: 3 -> 0, of which waited for: 2 -> 0; matrix products, arithmetic and copies ran while one was open for 17% -> 0% of each run, Pallas kernels for 0% -> 0%
where the time goes in v1:
time: 164 us
  Pallas kernels  156 us (95%)
  local copies, waits for them, and re-layouts  7 us (4%)
    pallas_call x1, Pallas kernels, per_device(): pl.pallas_call(kernel, out_shape=(jax.ShapeDtypeStruct((8 * 2 * B, R), F3...  156 us
    unnamed x2, local copies, waits for them, and re-layouts  5.7 us

profile of v1, /device:TPU:1, one launch (start us, length us, event | category | flops | bytes accessed | tf_op | source)
XLA Modules:
  0.0 163.9 jit_solution(14625467674665001946)
XLA Ops:
  0.6 3.0 %copy.11 = f32[128,2,16,96]{3,2,1,0:T(8,128)} copy(f32[128,2,16,96]{0,3,2,1:T(8,128)} %param.8) | data formatting | bytes 3145728 | tf_op args[0]
  3.6 156.3 %shard_map.95 = (f32[256,1536]{1,0:T(8,128)}, f32[8,128]{1,0:T(8,128)}) custom-call(f32[4096,96]{1,0:T(8,128)} %bitcast.4, f32[8192,32]{1,0:T(8,128)} %bitcast.5, s32[16,16]{1,0:T(8,128)} %fetch_ref.1, s32[4]{0:T(128)} %live_ref.1, f32[16]{0:T(128)} %r1_ref.1, f32[1,96]{1,0:T(1,128)} %bitcast.7, f32[12,128,128]{2,1,0:T(8,128)} %diag_ref.1, ...), custom_call_target="tpu_custom_call" | custom-call | tf_op jit(solution)/shard_map/pallas_call | solution.py:552
  159.9 1.3 slice_reduce_fusion
  161.2 2.7 %copy.13 = f32[8,2,16,1536]{3,2,1,0:T(8,128)} copy(f32[8,2,16,1536]{3,2,1,0:T(8,128)} %bitcast.6) | data formatting | bytes 3145728

commit v2 on v1

--- a/solution.py
+++ b/solution.py
@@ -18,8 +18,12 @@
 Q = 4
 CELLS = 768
 GS = 32
-T = 12
-GROUPS = 1 + T // 2
+T = 9
+GROUPS = 1 + (T + 1) // 2
+LAG = 2
+OCTETS = 16
+STATIC_T = 12
+STATIC_GROUPS = 1 + STATIC_T // 2
 LANES = 128
 PTS = 96
 
@@ -42,7 +46,7 @@
     return t0[:, 0:96], t1[:, 0:96], t2[:, 0:96], last
 
 
-def kernel(
+def static_kernel(
     state_ref,
     coup_ref,
     fetch_ref,
@@ -421,7 +425,7 @@
 
         @pl.when(q == 0)
         def _():
-            for group in range(4, GROUPS):
+            for group in range(4, STATIC_GROUPS):
                 build(group)
 
         sib_arrived(q, 2)
@@ -535,7 +539,7 @@
 
     @pl.loop(0, Q)
     def _(q):
-        for t in range(T):
+        for t in range(STATIC_T):
             for way in range(2):
                 ring_copy(q, t, way, ring_src(q, t, way)).wait_send()
             sib_copy(q, t).wait_send()
@@ -543,14 +547,14 @@
             coupled_copy(q, k).wait_send()
 
 
-def per_device(
+def static_program(
     state, coupling, fetch_group, live_slots, radius_one, radius_two, kinetic_diag, kinetic_link
 ):
     vmem = pl.BlockSpec(memory_space=pltpu.VMEM)
     smem = pl.BlockSpec(memory_space=pltpu.SMEM)
     dma = pltpu.SemaphoreType.DMA
     out, coef = pl.pallas_call(
-        kernel,
+        static_kernel,
         out_shape=(
             jax.ShapeDtypeStruct((8 * 2 * B, R), F32),
             jax.ShapeDtypeStruct((8, LANES), F32),
@@ -560,10 +564,10 @@
         scratch_shapes=[
             pltpu.VMEM((Q, 128, CELLS), F32),
             pltpu.VMEM((Q, 128, CELLS), F32),
-            pltpu.VMEM((Q, T * 4 * GS, CELLS), F32),
+            pltpu.VMEM((Q, STATIC_T * 4 * GS, CELLS), F32),
             pltpu.VMEM((Q, 6, GS, CELLS), F32),
-            pltpu.VMEM((GROUPS, 512, 256), BF16),
-            pltpu.VMEM((GROUPS, 512, 256), BF16),
+            pltpu.VMEM((STATIC_GROUPS, 512, 256), BF16),
+            pltpu.VMEM((STATIC_GROUPS, 512, 256), BF16),
             pltpu.VMEM((Q, 4, 8, CELLS), F32),
             pltpu.VMEM((512, CELLS), F32),
             pltpu.VMEM((Q, 128, CELLS), F32),
@@ -574,10 +578,10 @@
             pltpu.VMEM((R // LANES * 256, LANES), F32),
             pltpu.VMEM((2, 8, LANES), F32),
             pltpu.VMEM((2, DEV, 8, LANES), F32),
-            dma((2, Q, T)),
-            dma((2, Q, T)),
-            dma((Q, T)),
-            dma((Q, T)),
+            dma((2, Q, STATIC_T)),
+            dma((2, Q, STATIC_T)),
+            dma((Q, STATIC_T)),
+            dma((Q, STATIC_T)),
             dma((1,)),
             dma((1,)),
             dma((DEV,)),
@@ -588,7 +592,7 @@
             dma((2, DEV)),
         ],
         compiler_params=pltpu.CompilerParams(
-            collective_id=0, has_side_effects=True, vmem_limit_bytes=61 << 20
+            collective_id=1, has_side_effects=True, vmem_limit_bytes=61 << 20
         ),
     )(
         state.reshape(128 * 2 * B, PTS),
@@ -601,6 +605,810 @@
         kinetic_link,
     )
     return out.reshape(8, 2, B, R), coef[0:3, 0]
+
+
+def tie_up(v, dest_z, dest_core, source_core):
+    index = dest_z * 4 + dest_core * 2 + source_core
+    mixed = (((v * 5 + 3) * (index + 1) * (index + 7)) >> 3) & 1
+    odd = (dest_core + source_core) & 1
+    return jnp.where(
+        v == 0,
+        1 - odd,
+        jnp.where(v == 1, odd, jnp.where(v == 2, 1 - source_core, jnp.where(v == 3, source_core, mixed))),
+    )
+
+
+def flat4(t0, t1, t2):
+    return (
+        t0[:, 0:96],
+        jnp.concatenate([t0[:, 96:128], t1[:, 0:64]], axis=1),
+        jnp.concatenate([t1[:, 64:128], t2[:, 0:32]], axis=1),
+        t2[:, 32:128],
+    )
+
+
+def kernel(
+    state_hbm,
+    coup_hbm,
+    fetch_ref,
+    live_ref,
+    r1_ref,
+    r2_ref,
+    diag_hbm,
+    link_hbm,
+    out_ref,
+    coef_ref,
+    flag_ref,
+    state_v,
+    coup_v,
+    diag_v,
+    link_v,
+    xb,
+    pool,
+    stage,
+    ch,
+    cl,
+    wh,
+    wl,
+    kern,
+    acc,
+    cpl,
+    srecv,
+    crecv,
+    snat,
+    app,
+    rows_of,
+    part,
+    gath,
+    live_out,
+    live_in,
+    sim_key,
+    sim_read,
+    read_table,
+    slot_table,
+    load_sem,
+    live_send,
+    live_recv,
+    ring_send,
+    ring_recv,
+    sib_send,
+    sib_recv,
+    sx_send,
+    sx_recv,
+    st_send,
+    st_recv,
+    cp_send,
+    cp_recv,
+    sc_send,
+    sc_recv,
+):
+    me = lax.axis_index("chan")
+    rad = lax.axis_index("rad")
+    core = lax.rem(me, 2)
+    chip = me // 2
+    sib = me + 1 - 2 * core
+    up = (lax.rem(me + 2, DEV), rad)
+    down = (lax.rem(me + DEV - 2, DEV), rad)
+    sibling = (sib, rad)
+
+    def chan_peer(k):
+        return (lax.rem(me + k, DEV), rad)
+
+    def rad_peer(k):
+        return (me, lax.rem(rad + k, DEV))
+
+    loads = [
+        pltpu.make_async_copy(src, dst, load_sem.at[i])
+        for i, (src, dst) in enumerate(
+            ((state_hbm, state_v), (coup_hbm, coup_v), (diag_hbm, diag_v), (link_hbm, link_v))
+        )
+    ]
+    for load in loads:
+        load.start()
+    barrier = pltpu.get_barrier_semaphore()
+    for k in range(1, DEV):
+        pl.semaphore_signal(barrier, inc=1, device_id=chan_peer(k), device_id_type=MESH)
+        pl.semaphore_signal(barrier, inc=1, device_id=rad_peer(k), device_id_type=MESH)
+
+    mine = jnp.maximum(
+        jnp.maximum(live_ref[0], live_ref[1]), jnp.maximum(live_ref[2], live_ref[3])
+    )
+    live_out[...] = jnp.full((8, LANES), mine, jnp.int32)
+
+    lane = lax.broadcasted_iota(jnp.int32, (8, LANES), 1)
+    sub = lax.broadcasted_iota(jnp.int32, (8, LANES), 0)
+    lane_z = lane & 7
+    octet = lane >> 3
+    sub_core = sub >> 2
+    sub_block = sub & 3
+    spots = [[(lane_z == z) & (sub_core == s) for s in range(2)] for z in range(8)]
+    taken = {}
+    for delta in range(1, 8):
+        for dest_core in range(2):
+            value = jnp.zeros((8, LANES), jnp.int32)
+            for z in range(8):
+                for s in range(2):
+                    picked = fetch_ref[2 * ((z + delta) % 8) + dest_core, 2 * z + s]
+                    value = jnp.where(spots[z][s], picked, value)
+            taken[delta, dest_core] = value == sub_block
+
+    def live_copy(k):
+        return pltpu.make_async_remote_copy(
+            src_ref=live_out,
+            dst_ref=live_in.at[me],
+            send_sem=live_send.at[k],
+            recv_sem=live_recv.at[k],
+            device_id=chan_peer(k),
+            device_id_type=MESH,
+        )
+
+    def sibx_copy(q):
+        return pltpu.make_async_remote_copy(
+            src_ref=xb.at[core, q],
+            dst_ref=xb.at[core, q],
+            send_sem=sx_send.at[q],
+            recv_sem=sx_recv.at[q],
+            device_id=sibling,
+            device_id_type=MESH,
+        )
+
+    def state_copy(k):
+        return pltpu.make_async_remote_copy(
+            src_ref=xb.at[core, :, pl.ds(8 * lax.rem(rad + k, DEV), 8), :],
+            dst_ref=srecv.at[rad],
+            send_sem=st_send.at[k],
+            recv_sem=st_recv.at[k],
+            device_id=rad_peer(k),
+            device_id_type=MESH,
+        )
+
+    def coupled_copy(q, k):
+        return pltpu.make_async_remote_copy(
+            src_ref=cpl.at[q, pl.ds(8 * lax.rem(rad + k, DEV), 8), :],
+            dst_ref=crecv.at[q, rad],
+            send_sem=cp_send.at[q, k],
+            recv_sem=cp_recv.at[q, k],
+            device_id=rad_peer(k),
+            device_id_type=MESH,
+        )
+
+    def slot(t, side, way):
+        return pl.multiple_of((t * 4 + side * 2 + way) * GS, GS)
+
+    def ring_copy(q, t, way):
+        return pltpu.make_async_remote_copy(
+            src_ref=stage.at[way, q, t],
+            dst_ref=pool.at[q, pl.ds(slot(t, core, way), GS), :],
+            send_sem=ring_send.at[way, q, t],
+            recv_sem=ring_recv.at[way, q, t],
+            device_id=(up, down)[way],
+            device_id_type=MESH,
+        )
+
+    def sib_copy(q, t):
+        return pltpu.make_async_remote_copy(
+            src_ref=pool.at[q, pl.ds(slot(t, core, 0), 2 * GS), :],
+            dst_ref=pool.at[q, pl.ds(slot(t, core, 0), 2 * GS), :],
+            send_sem=sib_send.at[q, t],
+            recv_sem=sib_recv.at[q, t],
+            device_id=sibling,
+            device_id_type=MESH,
+        )
+
+    pl.semaphore_wait(barrier, 2 * (DEV - 1))
+    for k in range(1, DEV):
+        live_copy(k).start()
+    live_in[me] = live_out[...]
+
+    loads[0].wait()
+    for q in range(Q):
+        for plane in range(2):
+            rows = slice(plane * B * PTS + 384 * q, plane * B * PTS + 384 * q + 384)
+            xb[core, q, :, plane * 384 : plane * 384 + 384] = jnp.transpose(state_v[rows, :])
+        sibx_copy(q).start()
+    for k in range(1, DEV):
+        state_copy(k).start()
+    srecv[rad] = xb[core, :, pl.ds(pl.multiple_of(8 * rad, 8), 8), :]
+
+    for k in range(1, DEV):
+        live_copy(k).wait_recv()
+    most = []
+    for dest_core in range(2):
+        value = live_in[dest_core]
+        for z in range(1, 8):
+            value = jnp.where(lane_z == z, live_in[2 * z + dest_core], value)
+        most.append(value)
+
+    def turn(x, shift):
+        shift = shift % 8
+        if shift == 0:
+            return x
+        return jnp.where(
+            lane_z >= shift,
+            pltpu.roll(x, shift, 1),
+            pltpu.roll(x, LANES - 8 + shift, 1),
+        )
+
+    reach = []
+    for way in range(2):
+        value = jnp.zeros((8, LANES), jnp.int32)
+        for dist in range(1, 5):
+            delta = dist if way == 0 else 8 - dist
+            for dest_core in range(2):
+                k = ((2 * dist if way else -2 * dist) + sub_core - dest_core) & 15
+                need = taken[delta, dest_core] & (
+                    k < pltpu.roll(most[dest_core], LANES - delta, 1)
+                )
+                if dist == 4:
+                    upward = tie_up(octet, (lane_z + 4) & 7, dest_core, sub_core)
+                    need = need & (upward == 1 - way)
+                value = jnp.where(need, dist, value)
+        reach.append(value)
+
+    waiting, ready, where_from = [], [], []
+    for way in range(2):
+        here = [turn(reach[way], j if way == 0 else -j) for j in range(4)]
+        waiting.append(
+            [jnp.where(r > j, (r - j) * 32 + j * 8 + sub, 0) for j, r in enumerate(here)]
+        )
+        ready.append([jnp.full((8, LANES), 0 if j == 0 else 99, jnp.int32) for j in range(4)])
+        where_from.append([sub for _ in range(4)])
+
+    def peak(x):
+        for shift in (4, 2, 1):
+            x = jnp.maximum(x, pltpu.roll(x, shift, 0))
+        return x
+
+    sim_key[...] = jnp.zeros(sim_key.shape, jnp.int32)
+    sim_read[...] = jnp.zeros(sim_read.shape, jnp.int32)
+    for t in range(T):
+        for way in range(2):
+            wait, soon, source = waiting[way], ready[way], where_from[way]
+            sent = [jnp.zeros((8, LANES), jnp.int32) for _ in range(4)]
+            for side in range(2):
+                open_ = [
+                    jnp.where((soon[j] <= t) & (sent[j] == 0), wait[j], 0) for j in range(4)
+                ]
+                top = peak(functools.reduce(jnp.maximum, open_))
+                chosen = [(open_[j] == top) & (top > 0) for j in range(4)]
+                code = peak(
+                    functools.reduce(
+                        jnp.maximum,
+                        [jnp.where(chosen[j], source[j] + 1, 0) for j in range(4)],
+                    )
+                )
+                row = t * 4 + side * 2 + way
+                sim_key[row : row + 1, :] = top[0:1, :]
+                sim_read[row : row + 1, :] = code[0:1, :]
+                sent = [jnp.where(chosen[j], side + 1, sent[j]) for j in range(4)]
+            waiting[way] = [jnp.where(sent[j] > 0, 0, wait[j]) for j in range(4)]
+            for j in range(3):
+                came = turn(sent[j], 1 if way == 0 else -1)
+                soon[j + 1] = jnp.where(came > 0, t + LAG, soon[j + 1])
+                source[j + 1] = jnp.where(came > 0, 8 + 2 * t - 1 + came, source[j + 1])
+
+    left = peak(functools.reduce(jnp.maximum, waiting[0] + waiting[1]))
+    for shift in (4, 2, 1):
+        left = jnp.maximum(left, turn(left, shift))
+    routing = jnp.min(
+        jnp.where(left > 0, 99.0, octet.astype(F32)), axis=1, keepdims=True
+    )
+    flag_ref[0] = jnp.where(jnp.max(routing) > 50.0, 1, 0)
+    routing = jnp.where(routing > 50.0, 0.0, routing).astype(jnp.int32)[0:1, :]
+
+    rows_n = sim_key.shape[0]
+    wide = lax.broadcasted_iota(jnp.int32, (rows_n, LANES), 1)
+    tall = lax.broadcasted_iota(jnp.int32, (rows_n, LANES), 0)
+
+    def column(table, z):
+        hit = wide == routing * 8 + z
+        picked = jnp.where(hit, table.astype(F32), 0.0)
+        return jnp.broadcast_to(
+            jnp.sum(picked, axis=1, keepdims=True), (rows_n, LANES)
+        ).astype(jnp.int32)
+
+    read_table[...] = column(sim_read[...], chip)
+    came_way = tall & 1
+    key = column(
+        sim_key[...], jnp.where(came_way == 0, (chip + 7) & 7, (chip + 1) & 7)
+    )
+    ident = key & 31
+    dist = (ident >> 3) + 1
+    from_core = (ident >> 2) & 1
+    from_block = ident & 3
+    k = (jnp.where(came_way == 0, -2 * dist, 2 * dist) + from_core - core) & 15
+    fetched = jnp.zeros_like(k)
+    for j in range(DEV):
+        fetched = jnp.where(k == j, fetch_ref[me, lax.rem(me + j, DEV)], fetched)
+    upward = tie_up(jnp.broadcast_to(routing, (rows_n, LANES)), chip, core, from_core)
+    take = (key > 0) & (fetched == from_block) & (tall < 4 * T)
+    take = take & ((dist < 4) | (upward == 1 - came_way))
+    slot_table[8 : 8 + rows_n, :] = jnp.where(take, k, -1)
+    own = jnp.where(
+        sub_core == 0,
+        fetch_ref[me, me - core],
+        fetch_ref[me, me - core + 1],
+    )
+    slot_table[0:8, :] = jnp.where(own == sub_block, (sub_core - core) & 15, -1)
+
+    def ring_start(q, t):
+        for way in range(2):
+            row = t * 4 + way
+            code = jnp.where(
+                jnp.full((1, LANES), core, jnp.int32) == 0,
+                read_table[row : row + 1, :],
+                read_table[row + 2 : row + 3, :],
+            )
+            code = jnp.broadcast_to(code, (GS, LANES))
+            tiles = [slice(i * LANES, i * LANES + LANES) for i in range(6)]
+            chosen = [xb[0, q, 0:GS, c] for c in tiles]
+            for i in range(1, 8 + 2 * max(0, t - LAG + 1)):
+                hit = code == i + 1
+                for n, c in enumerate(tiles):
+                    if i < 8:
+                        rows = pl.ds((i % 4) * GS, GS)
+                        block = xb[i // 4, q, rows, c]
+                    else:
+                        block = pool[q, pl.ds(slot((i - 8) // 2, i % 2, way), GS), c]
+                    chosen[n] = jnp.where(hit, block, chosen[n])
+            for n, c in enumerate(tiles):
+                stage[way, q, t, :, c] = chosen[n]
+            ring_copy(q, t, way).start()
+
+    def ring_arrived(q, t):
+        for way in range(2):
+            ring_copy(q, t, way).wait_recv()
+        sib_copy(q, t).start()
+
+    def sib_arrived(q, t):
+        sib_copy(q, t).wait_recv()
+
+    def build_coupling():
+        loads[1].wait()
+        for g in range(4):
+            for four in range(4):
+                on = [
+                    jnp.where(live_ref[g] > 4 * four + j, 1.0, 0.0) for j in range(4)
+                ]
+                for order in range(4):
+                    block = jnp.concatenate(
+                        [
+                            coup_v[pl.ds(((g * 16 + 4 * four + j) * 4 + order) * GS, GS), :]
+                            * on[j]
+                            for j in range(4)
+                        ],
+                        axis=1,
+                    )
+                    high, low = split(block)
+                    rows = slice(order * 128 + g * GS, order * 128 + g * GS + GS)
+                    cols = slice(four * LANES, four * LANES + LANES)
+                    ch[rows, cols] = high
+                    cl[rows, cols] = low
+
+    def build(group):
+        width = 256 if group < GROUPS - 1 or T % 2 == 0 else 128
+        depth = lax.broadcasted_iota(jnp.int32, (512, LANES), 0)
+        across = lax.broadcasted_iota(jnp.int32, (1, LANES), 1)
+        for half in range(width // 128):
+            target = jnp.full((1, LANES), -1, jnp.int32)
+            for p in range(4):
+                row = 8 * group + 4 * half + p
+                target = jnp.where(across >> 5 == p, slot_table[row : row + 1, :], target)
+            target = target * GS + (across & 31)
+            select = jnp.where(depth == target, 1.0, 0.0).astype(BF16)
+            cols = slice(half * 128, half * 128 + 128)
+            for src, dst in ((ch, wh), (cl, wl)):
+                dst[group, :, cols] = jnp.dot(
+                    src[...], select, preferred_element_type=F32
+                ).astype(BF16)
+
+    def compute(q, group):
+        half = lax.rem(q, 2)
+        width = 256 if group < GROUPS - 1 or T % 2 == 0 else 128
+
+        @pl.loop(0, 3)
+        def _(j):
+            at = pl.multiple_of(j * 256, 256)
+            if group == 0:
+                x = jnp.concatenate(
+                    [xb[0, q, :, pl.ds(at, 256)], xb[1, q, :, pl.ds(at, 256)]], axis=0
+                )
+            else:
+                x = pool[q, pl.ds(256 * (group - 1), width), pl.ds(at, 256)]
+            xh, xl = split(x)
+            dot = functools.partial(jnp.dot, preferred_element_type=F32)
+            gh, gl = wh[group, :, 0:width], wl[group, :, 0:width]
+            total = dot(gh, xh) + dot(gl, xh) + dot(gh, xl)
+            if group == 0:
+                acc[half, :, pl.ds(at, 256)] = total
+            else:
+                acc[half, :, pl.ds(at, 256)] += total
+
+    def build_kern():
+        row = jnp.broadcast_to(r2_ref[0:1, :], (8, PTS))
+        flat = jnp.concatenate([row] * 4, axis=1)
+        point = lax.broadcasted_iota(jnp.int32, (8, 384), 1)
+        for q in range(Q):
+            one = jnp.where(
+                point < PTS,
+                r1_ref[4 * q],
+                jnp.where(
+                    point < 2 * PTS,
+                    r1_ref[4 * q + 1],
+                    jnp.where(point < 3 * PTS, r1_ref[4 * q + 2], r1_ref[4 * q + 3]),
+                ),
+            )
+            nearer = jnp.minimum(one, flat)
+            farther = jnp.maximum(one, flat)
+            top = jnp.ones_like(nearer)
+            bottom = farther
+            for order in range(4):
+                value = top / bottom
+                kern[q, order, :, 0:384] = value
+                kern[q, order, :, 384:768] = value
+                top = top * nearer
+                bottom = bottom * farther
+
+    def finish_chunk(q):
+        half = lax.rem(q, 2)
+        for tile in range(6):
+            cols = slice(tile * LANES, tile * LANES + LANES)
+            total = jnp.zeros((128, LANES), F32)
+            for order in range(4):
+                factor = jnp.broadcast_to(kern[q, order, 0:1, cols], (128, LANES))
+                total = total + acc[half, order * 128 : order * 128 + 128, cols] * factor
+            cpl[q, :, cols] = total
+        for k in range(1, DEV):
+            coupled_copy(q, k).start()
+        crecv[q, rad] = cpl[q, pl.ds(pl.multiple_of(8 * rad, 8), 8), :]
+
+    def natural(piece):
+        out = []
+        for plane in range(2):
+            cols = [slice((plane * 3 + i) * LANES, (plane * 3 + i + 1) * LANES) for i in range(3)]
+            parts = [flat4(*(piece(s, c) for c in cols)) for s in range(4)]
+            for i in range(4):
+                out.append(jnp.concatenate([p[i] for p in parts], axis=1))
+        return out
+
+    def receive_state():
+        for k in range(1, DEV):
+            state_copy(k).wait_recv()
+        for q in range(Q):
+            for quad in range(4):
+                for i, value in enumerate(
+                    natural(lambda s, c: srecv[4 * quad + s, q, :, c])
+                ):
+                    rows = slice(q * 64 + i * 8, q * 64 + i * 8 + 8)
+                    snat[rows, 384 * quad : 384 * quad + 384] = value
+
+    def kinetic(elements):
+        high = functools.partial(
+            lax.dot_general, precision=lax.Precision.HIGHEST, preferred_element_type=F32
+        )
+        same = (((1,), (1,)), ((), ()))
+        flip = (((1,), (0,)), ((), ()))
+        for e in elements:
+            cols = [slice(128 * x, 128 * x + 128) for x in (e - 1, e, e + 1)]
+            value = high(snat[:, cols[1]], diag_v[e], same)
+            if e > 0:
+                value = value + high(snat[:, cols[0]], link_v[e - 1], same)
+            if e < 11:
+                value = value + high(snat[:, cols[2]], link_v[e], flip)
+            app[:, cols[1]] = value
+
+    def receive_coupled(q):
+        for k in range(1, DEV):
+            coupled_copy(q, k).wait_recv()
+        for quad in range(4):
+            for i, value in enumerate(
+                natural(lambda s, c: crecv[q, 4 * quad + s, :, c])
+            ):
+                rows = pl.ds(pl.multiple_of(q * 64 + i * 8, 8), 8)
+                cols = slice(384 * quad, 384 * quad + 384)
+                app[rows, cols] += value
+
+    for q in range(Q):
+        sibx_copy(q).wait_recv()
+
+    def chunk_round(n):
+        return 2 * (n // (2 * T)) + lax.rem(n, 2), lax.rem(n, 2 * T) // 2
+
+    @pl.loop(0, Q // 2)
+    def _(pair):
+        for t in range(T):
+
+            @pl.loop(0, 2)
+            def _(parity):
+                q = 2 * pair + parity
+                last = q - 2
+                n = 2 * T * pair + 2 * t + parity
+
+                @pl.when(n >= 3)
+                def _():
+                    ring_arrived(*chunk_round(n - 3))
+
+                @pl.when(n >= 4)
+                def _():
+                    sib_arrived(*chunk_round(n - 4))
+
+                ring_start(q, t)
+
+                if t == 0:
+
+                    @pl.when(q == 0)
+                    def _():
+                        build_coupling()
+
+                if t == 1:
+
+                    @pl.when(q == 0)
+                    def _():
+                        build(0)
+                        build(1)
+
+                    @pl.when(q == 1)
+                    def _():
+                        build_kern()
+
+                if t < LAG and (T + t) % 2 and (T + t) // 2 < GROUPS - 1:
+
+                    @pl.when(q > 1)
+                    def _():
+                        compute(last, (T + t) // 2)
+
+                if t == 1:
+
+                    @pl.when(q > 1)
+                    def _():
+                        compute(last, GROUPS - 1)
+                        finish_chunk(last)
+
+                if t == 2:
+                    compute(q, 0)
+                if t > LAG and t % 2 and t // 2 < GROUPS - 1:
+                    compute(q, t // 2)
+                if t == 4:
+
+                    @pl.when(q == 0)
+                    def _():
+                        build(2)
+
+                    @pl.when(q == 1)
+                    def _():
+                        build(3)
+
+                if t == 6:
+
+                    @pl.when(q == 0)
+                    def _():
+                        for group in range(4, GROUPS):
+                            build(group)
+
+                    @pl.when(q == 1)
+                    def _():
+                        receive_state()
+
+                    @pl.when(q > 1)
+                    def _():
+                        receive_coupled(last)
+
+                if t == T - 1:
+
+                    @pl.when(q == 0)
+                    def _():
+                        loads[2].wait()
+                        loads[3].wait()
+                        kinetic(range(0, 6))
+
+                    @pl.when(q == 1)
+                    def _():
+                        kinetic(range(6, 12))
+
+    steps = Q * T
+    ring_arrived(*chunk_round(steps - 3))
+    sib_arrived(*chunk_round(steps - 4))
+    ring_arrived(*chunk_round(steps - 2))
+    sib_arrived(*chunk_round(steps - 3))
+    if T % 2:
+        compute(Q - 2, GROUPS - 2)
+        compute(Q - 1, GROUPS - 2)
+    sib_arrived(*chunk_round(steps - 2))
+    compute(Q - 2, GROUPS - 1)
+    finish_chunk(Q - 2)
+    ring_arrived(*chunk_round(steps - 1))
+    sib_arrived(*chunk_round(steps - 1))
+    compute(Q - 1, GROUPS - 1)
+    finish_chunk(Q - 1)
+    receive_coupled(Q - 2)
+    receive_coupled(Q - 1)
+
+    def parts(q):
+        re = pl.ds(q * 64, 32)
+        im = pl.ds(q * 64 + 32, 32)
+        return snat[re, :], snat[im, :], app[re, :], app[im, :]
+
+    def fold(x):
+        return jnp.sum(x, axis=0, keepdims=True)
+
+    sums = [jnp.zeros((1, R), F32) for _ in range(3)]
+    for q in range(Q):
+        sre, sim, are, aim = parts(q)
+        sums[0] += fold(sre * aim - sim * are)
+        sums[1] -= fold(sre * are + sim * aim)
+        sums[2] += fold(sre * sre + sim * sim)
+    cross_re, cross_im, self_sq = (jnp.sum(x, axis=1, keepdims=True) for x in sums)
+
+    def ratio(x, y):
+        return jnp.where(y > 0.0, x / jnp.where(y > 0.0, y, 1.0), 0.0)
+
+    own_re, own_im = ratio(cross_re, self_sq), ratio(cross_im, self_sq)
+    left = jnp.zeros((1, R), F32)
+    for q in range(Q):
+        sre, sim, are, aim = parts(q)
+        ore = aim - (own_re * sre - own_im * sim)
+        oim = -are - (own_re * sim + own_im * sre)
+        left += fold(ore * ore + oim * oim)
+    left = jnp.sum(left, axis=1, keepdims=True)
+    for i, value in enumerate((cross_re, cross_im, self_sq, left)):
+        part[0, i : i + 1, :] = jnp.broadcast_to(value, (1, LANES))
+
+    def scalar_copy(stage_, k):
+        return pltpu.make_async_remote_copy(
+            src_ref=part.at[stage_],
+            dst_ref=gath.at[stage_, (me, rad)[stage_]],
+            send_sem=sc_send.at[stage_, k],
+            recv_sem=sc_recv.at[stage_, k],
+            device_id=(chan_peer, rad_peer)[stage_](k),
+            device_id_type=MESH,
+        )
+
+    def merge(stage_):
+        for k in range(1, DEV):
+            scalar_copy(stage_, k).start()
+        gath[stage_, (me, rad)[stage_]] = part[stage_]
+        for k in range(1, DEV):
+            scalar_copy(stage_, k).wait_recv()
+        rows = [[gath[stage_, j, i : i + 1, :] for j in range(DEV)] for i in range(4)]
+        add = lambda xs: functools.reduce(lambda x, y: x + y, xs)
+        cre, cim, sq = add(rows[0]), add(rows[1]), add(rows[2])
+        pre, pim = ratio(cre, sq), ratio(cim, sq)
+        rest = add(rows[3])
+        for j in range(DEV):
+            dre = pre - ratio(rows[0][j], rows[2][j])
+            dim = pim - ratio(rows[1][j], rows[2][j])
+            rest = rest + (dre * dre + dim * dim) * rows[2][j]
+        return cre, cim, sq, rest, pre, pim
+
+    merged = merge(0)
+    for i in range(4):
+        part[1, i : i + 1, :] = merged[i]
+    _, _, _, rest, pre, pim = merge(1)
+    rms = jnp.sqrt(rest / (2.0 * C * B * R) + 1e-06)
+    place = lax.broadcasted_iota(jnp.int32, (1, 3), 1)
+    coef_ref[...] = jnp.where(
+        place == 0, pre[:, 0:3], jnp.where(place == 1, pim[:, 0:3], rms[:, 0:3])
+    )
+    pre1, pim1 = pre[:, 0:1], pim[:, 0:1]
+    for q in range(Q):
+        for i in range(4):
+            re = slice(q * 64 + i * 8, q * 64 + i * 8 + 8)
+            im = slice(q * 64 + 32 + i * 8, q * 64 + 32 + i * 8 + 8)
+            sre, sim, are, aim = snat[re, :], snat[im, :], app[re, :], app[im, :]
+            ore = aim - (pre1 * sre - pim1 * sim)
+            oim = -are - (pre1 * sim + pim1 * sre)
+            for tile in range(R // LANES):
+                cols = slice(tile * LANES, tile * LANES + LANES)
+                rows = tile * 256 + 4 * q + i
+                rows_of[pl.ds(rows, 8, stride=2 * B), :] = ore[:, cols]
+                rows_of[pl.ds(rows + B, 8, stride=2 * B), :] = oim[:, cols]
+    for tile in range(R // LANES):
+        out_ref[:, tile * LANES : tile * LANES + LANES] = rows_of[tile * 256 : tile * 256 + 256, :]
+
+    for k in range(1, DEV):
+        live_copy(k).wait_send()
+        state_copy(k).wait_send()
+        scalar_copy(0, k).wait_send()
+        scalar_copy(1, k).wait_send()
+
+    @pl.loop(0, Q)
+    def _(q):
+        sibx_copy(q).wait_send()
+        for t in range(T):
+            for way in range(2):
+                ring_copy(q, t, way).wait_send()
+            sib_copy(q, t).wait_send()
+        for k in range(1, DEV):
+            coupled_copy(q, k).wait_send()
+
+
+def per_device(
+    state, coupling, fetch_group, live_slots, radius_one, radius_two, kinetic_diag, kinetic_link
+):
+    vmem = pl.BlockSpec(memory_space=pltpu.VMEM)
+    smem = pl.BlockSpec(memory_space=pltpu.SMEM)
+    hbm = pl.BlockSpec(memory_space=pl.ANY)
+    dma = pltpu.SemaphoreType.DMA
+    rows_n = -(-4 * T // 8) * 8
+    out, coef, flag = pl.pallas_call(
+        kernel,
+        out_shape=(
+            jax.ShapeDtypeStruct((8 * 2 * B, R), F32),
+            jax.ShapeDtypeStruct((1, 3), F32),
+            jax.ShapeDtypeStruct((1,), jnp.int32),
+        ),
+        in_specs=[hbm, hbm, smem, smem, smem, vmem, hbm, hbm],
+        out_specs=(vmem, vmem, smem),
+        scratch_shapes=[
+            pltpu.VMEM((2 * B * PTS, 128), F32),
+            pltpu.VMEM((4 * 16 * 4 * GS, GS), F32),
+            pltpu.VMEM((12, 128, 128), F32),
+            pltpu.VMEM((11, 128, 128), F32),
+            pltpu.VMEM((2, Q, 128, CELLS), F32),
+            pltpu.VMEM((Q, T * 4 * GS, CELLS), F32),
+            pltpu.VMEM((2, Q, T, GS, CELLS), F32),
+            pltpu.VMEM((512, 512), BF16),
+            pltpu.VMEM((512, 512), BF16),
+            pltpu.VMEM((GROUPS, 512, 256), BF16),
+            pltpu.VMEM((GROUPS, 512, 256), BF16),
+            pltpu.VMEM((Q, 4, 8, CELLS), F32),
+            pltpu.VMEM((2, 512, CELLS), F32),
+            pltpu.VMEM((Q, 128, CELLS), F32),
+            pltpu.VMEM((DEV, Q, 8, CELLS), F32),
+            pltpu.VMEM((Q, DEV, 8, CELLS), F32),
+            pltpu.VMEM((256, R), F32),
+            pltpu.VMEM((256, R), F32),
+            pltpu.VMEM((R // LANES * 256, LANES), F32),
+            pltpu.VMEM((2, 8, LANES), F32),
+            pltpu.VMEM((2, DEV, 8, LANES), F32),
+            pltpu.VMEM((8, LANES), jnp.int32),
+            pltpu.VMEM((DEV, 8, LANES), jnp.int32),
+            pltpu.VMEM((rows_n, LANES), jnp.int32),
+            pltpu.VMEM((rows_n, LANES), jnp.int32),
+            pltpu.VMEM((rows_n, LANES), jnp.int32),
+            pltpu.VMEM((8 + rows_n, LANES), jnp.int32),
+            dma((4,)),
+            dma((DEV,)),
+            dma((DEV,)),
+            dma((2, Q, T)),
+            dma((2, Q, T)),
+            dma((Q, T)),
+            dma((Q, T)),
+            dma((Q,)),
+            dma((Q,)),
+            dma((DEV,)),
+            dma((DEV,)),
+            dma((Q, DEV)),
+            dma((Q, DEV)),
+            dma((2, DEV)),
+            dma((2, DEV)),
+        ],
+        compiler_params=pltpu.CompilerParams(
+            collective_id=0, has_side_effects=True, vmem_limit_bytes=61 << 20
+        ),
+    )(
+        state.transpose(1, 2, 3, 0).reshape(2 * B * PTS, 128),
+        coupling.reshape(4 * 16 * 4 * GS, GS),
+        fetch_group,
+        live_slots,
+        radius_one,
+        radius_two.reshape(1, PTS),
+        kinetic_diag,
+        kinetic_link,
+    )
+    return lax.cond(
+        flag[0] > 0,
+        static_program,
+        lambda *_: (out.reshape(8, 2, B, R), coef.reshape(3)),
+        state,
+        coupling,
+        fetch_group,
+        live_slots,
+        radius_one,
+        radius_two,
+        kinetic_diag,
+        kinetic_link,
+    )
 
 
 def solution(mesh):

time: 164 us -> 133 us (0.81)
  Pallas kernels: 156 us -> 128 us
  local copies, waits for them, and re-layouts: 7 us -> 3.22 us
    pallas_call x1, Pallas kernels: 156 us -> 128 us  [per_device(): pl.pallas_call(kernel, out_shape=(jax.ShapeDtypeStruct((8 * 2 * B, R), F3...]
    unnamed x2 -> x10, local copies, waits for them, and re-layouts: 5.7 us -> 3.22 us
where the time goes in v2:
time: 133 us
  Pallas kernels  128 us (96%)
  local copies, waits for them, and re-layouts  3.22 us (2%)
    pallas_call x1, Pallas kernels, per_device(): pl.pallas_call(kernel, out_shape=(jax.ShapeDtypeStruct((8 * 2 * B, R), F3...  128 us
    unnamed x10, local copies, waits for them, and re-layouts  3.22 us

profile of v2, /device:TPU:1, one launch (start us, length us, event | category | flops | bytes accessed | tf_op | source)
XLA Modules:
  0.0 132.9 jit_solution(4500952128583462527)
XLA Ops:
  0.6 0.0 copy-start
  0.6 0.0 copy-start.1
  0.6 0.0 copy-start.2
  0.7 128.1 %shard_map.95 = (f32[256,1536]{1,0:T(8,128)}, f32[1,3]{1,0:T(1,128)}, s32[1]{0:T(128)}) custom-call(f32[3072,128]{1,0:T(8,128)} %bitcast.14, f32[8192,32]{1,0:T(8,128)} %bitcast.11, s32[16,16]{1,0:T(8,128)} %fetch_ref.1, s32[4]{0:T(128)} %live_ref.1, f32[16]{0:T(128)} %r1_ref.1, f32[1,96]{1,0:T(1,128)} %bitcast.16, f32[12,128,128]{2,1,0:T(8,128)} %diag_hbm.1, ...), custom_call_target="tpu_custom_call" | custom-call | tf_op jit(solution)/shard_map/pallas_call | solution.py:1333
  129.3 0.0 copy-done
  129.4 0.0 copy-done.1
  129.4 0.0 copy-done.2
  129.4 0.3 conditional.1
  129.6 0.0 copy-start.3
  129.7 2.7 %copy.18 = f32[8,2,16,1536]{3,2,1,0:T(8,128)} copy(f32[8,2,16,1536]{3,2,1,0:T(8,128)} %bitcast.15) | data formatting | bytes 3145728
  132.4 0.0 copy-done.3
  132.4 0.5 copy.19
Async XLA Ops:
  0.6 128.7 %copy-start = (f32[128,2,16,96]{0,3,2,1:T(8,128)S(1)}, f32[128,2,16,96]{0,3,2,1:T(8,128)}, u32[]{:S(2)}) copy-start(f32[128,2,16,96]{0,3,2,1:T(8,128)} %param.10) | copy-start | bytes 4718596
  0.6 128.7 %copy-start.1 = (f32[12,128,128]{2,1,0:T(8,128)S(1)}, f32[12,128,128]{2,1,0:T(8,128)}, u32[]{:S(2)}) copy-start(f32[12,128,128]{2,1,0:T(8,128)} %diag_hbm.1) | copy-start | bytes 2359300
  0.6 128.7 %copy-start.2 = (f32[11,128,128]{2,1,0:T(8,128)S(1)}, f32[11,128,128]{2,1,0:T(8,128)}, u32[]{:S(2)}) copy-start(f32[11,128,128]{2,1,0:T(8,128)} %link_hbm.1) | copy-start | bytes 2162692
  129.6 2.7 %copy-start.3 = (f32[3]{0:T(128)S(1)}, f32[3]{0:T(128)}, u32[]{:S(2)}) copy-start(f32[3]{0:T(128)} %get-tuple-element.67) | copy-start | bytes 40

commit v3 on v2

--- a/solution.py
+++ b/solution.py
@@ -655,9 +655,12 @@
     cpl,
     srecv,
     crecv,
-    snat,
-    app,
-    rows_of,
+    s_nat,
+    k_nat,
+    a_nat,
+    kout,
+    krecv,
+    stat,
     part,
     gath,
     live_out,
@@ -679,6 +682,8 @@
     st_recv,
     cp_send,
     cp_recv,
+    kn_send,
+    kn_recv,
     sc_send,
     sc_recv,
 ):
@@ -1049,7 +1054,7 @@
                 top = top * nearer
                 bottom = bottom * farther
 
-    def finish_chunk(q):
+    def fold_orders(q):
         half = lax.rem(q, 2)
         for tile in range(6):
             cols = slice(tile * LANES, tile * LANES + LANES)
@@ -1058,9 +1063,41 @@
                 factor = jnp.broadcast_to(kern[q, order, 0:1, cols], (128, LANES))
                 total = total + acc[half, order * 128 : order * 128 + 128, cols] * factor
             cpl[q, :, cols] = total
+
+    def kinetic_copy(k):
+        return pltpu.make_async_remote_copy(
+            src_ref=kout.at[lax.rem(rad + k, DEV)],
+            dst_ref=krecv.at[:, pl.ds(8 * rad, 8), :],
+            send_sem=kn_send.at[k],
+            recv_sem=kn_recv.at[k],
+            device_id=rad_peer(k),
+            device_id_type=MESH,
+        )
+
+    def fold(x):
+        return jnp.sum(jnp.sum(x, axis=0, keepdims=True), axis=1, keepdims=True)
+
+    def ratio(x, y):
+        return jnp.where(y > 0.0, x / jnp.where(y > 0.0, y, 1.0), 0.0)
+
+    def send_chunk(q):
+        for tile in range(6):
+            cols = slice(tile * LANES, tile * LANES + LANES)
+            cpl[q, :, cols] += krecv[q, :, cols]
         for k in range(1, DEV):
             coupled_copy(q, k).start()
         crecv[q, rad] = cpl[q, pl.ds(pl.multiple_of(8 * rad, 8), 8), :]
+        sre, sim = xb[core, q, :, 0:384], xb[core, q, :, 384:768]
+        are, aim = cpl[q, :, 0:384], cpl[q, :, 384:768]
+        cross_re = fold(sre * aim - sim * are)
+        cross_im = -fold(sre * are + sim * aim)
+        self_sq = fold(sre * sre + sim * sim)
+        own_re, own_im = ratio(cross_re, self_sq), ratio(cross_im, self_sq)
+        ore = aim - (own_re * sre - own_im * sim)
+        oim = -are - (own_re * sim + own_im * sre)
+        left = fold(ore * ore + oim * oim)
+        for i, value in enumerate((cross_re, cross_im, self_sq, left)):
+            stat[q, i : i + 1, :] = jnp.broadcast_to(value, (1, LANES))
 
     def natural(piece):
         out = []
@@ -1071,16 +1108,21 @@
                 out.append(jnp.concatenate([p[i] for p in parts], axis=1))
         return out
 
+    def lay(target, q, quad, values):
+        for i, value in enumerate(values):
+            row = (i // 4) * B + 4 * q + i % 4
+            for j in range(3):
+                at = (3 * quad + j) * 256 + row
+                target[pl.ds(at, 8, stride=2 * B), :] = value[:, j * LANES : j * LANES + LANES]
+
     def receive_state():
         for k in range(1, DEV):
             state_copy(k).wait_recv()
-        for q in range(Q):
+
+        @pl.loop(0, Q)
+        def _(q):
             for quad in range(4):
-                for i, value in enumerate(
-                    natural(lambda s, c: srecv[4 * quad + s, q, :, c])
-                ):
-                    rows = slice(q * 64 + i * 8, q * 64 + i * 8 + 8)
-                    snat[rows, 384 * quad : 384 * quad + 384] = value
+                lay(s_nat, q, quad, natural(lambda s, c: srecv[4 * quad + s, q, :, c]))
 
     def kinetic(elements):
         high = functools.partial(
@@ -1089,24 +1131,47 @@
         same = (((1,), (1,)), ((), ()))
         flip = (((1,), (0,)), ((), ()))
         for e in elements:
-            cols = [slice(128 * x, 128 * x + 128) for x in (e - 1, e, e + 1)]
-            value = high(snat[:, cols[1]], diag_v[e], same)
+            here = [slice(256 * x, 256 * x + 256) for x in (e - 1, e, e + 1)]
+            value = high(s_nat[here[1], :], diag_v[e], same)
             if e > 0:
-                value = value + high(snat[:, cols[0]], link_v[e - 1], same)
+                value = value + high(s_nat[here[0], :], link_v[e - 1], same)
             if e < 11:
-                value = value + high(snat[:, cols[2]], link_v[e], flip)
-            app[:, cols[1]] = value
+                value = value + high(s_nat[here[2], :], link_v[e], flip)
+            k_nat[here[1], :] = value
+
+    def send_kinetic():
+        @pl.loop(0, Q)
+        def _(q):
+            for plane in range(2):
+                for quad in range(4):
+                    rows = [
+                        jnp.concatenate(
+                            [
+                                k_nat[
+                                    pl.ds((3 * quad + j) * 256 + plane * B + 4 * q + i, 8, stride=2 * B),
+                                    :,
+                                ]
+                                for j in range(3)
+                            ],
+                            axis=1,
+                        )
+                        for i in range(4)
+                    ]
+                    for s in range(4):
+                        kout[4 * quad + s, q, :, plane * 384 : plane * 384 + 384] = jnp.concatenate(
+                            [flat4(*(r[:, c * LANES : c * LANES + LANES] for c in range(3)))[s] for r in rows],
+                            axis=1,
+                        )
+
+        for k in range(1, DEV):
+            kinetic_copy(k).start()
+        krecv[:, pl.ds(pl.multiple_of(8 * rad, 8), 8), :] = kout[rad]
 
     def receive_coupled(q):
         for k in range(1, DEV):
             coupled_copy(q, k).wait_recv()
         for quad in range(4):
-            for i, value in enumerate(
-                natural(lambda s, c: crecv[q, 4 * quad + s, :, c])
-            ):
-                rows = pl.ds(pl.multiple_of(q * 64 + i * 8, 8), 8)
-                cols = slice(384 * quad, 384 * quad + 384)
-                app[rows, cols] += value
+            lay(a_nat, q, quad, natural(lambda s, c: crecv[q, 4 * quad + s, :, c]))
 
     for q in range(Q):
         sibx_copy(q).wait_recv()
@@ -1162,7 +1227,7 @@
                     @pl.when(q > 1)
                     def _():
                         compute(last, GROUPS - 1)
-                        finish_chunk(last)
+                        fold_orders(last)
 
                 if t == 2:
                     compute(q, 0)
@@ -1173,27 +1238,13 @@
                     @pl.when(q == 0)
                     def _():
                         build(2)
-
-                    @pl.when(q == 1)
-                    def _():
                         build(3)
-
-                if t == 6:
-
-                    @pl.when(q == 0)
-                    def _():
-                        for group in range(4, GROUPS):
-                            build(group)
 
                     @pl.when(q == 1)
                     def _():
                         receive_state()
 
-                    @pl.when(q > 1)
-                    def _():
-                        receive_coupled(last)
-
-                if t == T - 1:
+                if t == 5:
 
                     @pl.when(q == 0)
                     def _():
@@ -1204,6 +1255,32 @@
                     @pl.when(q == 1)
                     def _():
                         kinetic(range(6, 12))
+
+                    @pl.when(q == 2)
+                    def _():
+                        for k in range(1, DEV):
+                            kinetic_copy(k).wait_recv()
+
+                    @pl.when(q > 1)
+                    def _():
+                        send_chunk(last)
+
+                if t == 6:
+
+                    @pl.when(q == 0)
+                    def _():
+                        send_kinetic()
+
+                    @pl.when(q == 1)
+                    def _():
+                        for group in range(4, GROUPS):
+                            build(group)
+
+                if t == T - 1:
+
+                    @pl.when(q > 1)
+                    def _():
+                        receive_coupled(last)
 
     steps = Q * T
     ring_arrived(*chunk_round(steps - 3))
@@ -1215,99 +1292,74 @@
         compute(Q - 1, GROUPS - 2)
     sib_arrived(*chunk_round(steps - 2))
     compute(Q - 2, GROUPS - 1)
-    finish_chunk(Q - 2)
+    fold_orders(Q - 2)
+    send_chunk(Q - 2)
     ring_arrived(*chunk_round(steps - 1))
     sib_arrived(*chunk_round(steps - 1))
     compute(Q - 1, GROUPS - 1)
-    finish_chunk(Q - 1)
+    fold_orders(Q - 1)
+    send_chunk(Q - 1)
+
+    def merge(groups):
+        rows = [[g[i] for g in groups] for i in range(4)]
+        cre, cim, sq, rest = (functools.reduce(lambda x, y: x + y, r) for r in rows)
+        pre, pim = ratio(cre, sq), ratio(cim, sq)
+        for gre, gim, gsq, _ in groups:
+            dre = pre - ratio(gre, gsq)
+            dim = pim - ratio(gim, gsq)
+            rest = rest + (dre * dre + dim * dim) * gsq
+        return cre, cim, sq, rest, pre, pim
+
+    def group_of(ref):
+        return [ref[i : i + 1, :] for i in range(4)]
+
+    def scalar_copy(hop, k):
+        return pltpu.make_async_remote_copy(
+            src_ref=part.at[hop],
+            dst_ref=gath.at[hop, (me, rad)[hop]],
+            send_sem=sc_send.at[hop, k],
+            recv_sem=sc_recv.at[hop, k],
+            device_id=(chan_peer, rad_peer)[hop](k),
+            device_id_type=MESH,
+        )
+
+    def put(hop, merged):
+        for i in range(4):
+            part[hop, i : i + 1, :] = merged[i]
+        for k in range(1, DEV):
+            scalar_copy(hop, k).start()
+        gath[hop, (me, rad)[hop]] = part[hop]
+
+    def take_all(hop):
+        for k in range(1, DEV):
+            scalar_copy(hop, k).wait_recv()
+        return merge([group_of(gath.at[hop, j]) for j in range(DEV)])
+
+    part[...] = jnp.zeros(part.shape, F32)
+    put(0, merge([group_of(stat.at[q]) for q in range(Q)]))
+    put(1, take_all(0))
     receive_coupled(Q - 2)
     receive_coupled(Q - 1)
-
-    def parts(q):
-        re = pl.ds(q * 64, 32)
-        im = pl.ds(q * 64 + 32, 32)
-        return snat[re, :], snat[im, :], app[re, :], app[im, :]
-
-    def fold(x):
-        return jnp.sum(x, axis=0, keepdims=True)
-
-    sums = [jnp.zeros((1, R), F32) for _ in range(3)]
-    for q in range(Q):
-        sre, sim, are, aim = parts(q)
-        sums[0] += fold(sre * aim - sim * are)
-        sums[1] -= fold(sre * are + sim * aim)
-        sums[2] += fold(sre * sre + sim * sim)
-    cross_re, cross_im, self_sq = (jnp.sum(x, axis=1, keepdims=True) for x in sums)
-
-    def ratio(x, y):
-        return jnp.where(y > 0.0, x / jnp.where(y > 0.0, y, 1.0), 0.0)
-
-    own_re, own_im = ratio(cross_re, self_sq), ratio(cross_im, self_sq)
-    left = jnp.zeros((1, R), F32)
-    for q in range(Q):
-        sre, sim, are, aim = parts(q)
-        ore = aim - (own_re * sre - own_im * sim)
-        oim = -are - (own_re * sim + own_im * sre)
-        left += fold(ore * ore + oim * oim)
-    left = jnp.sum(left, axis=1, keepdims=True)
-    for i, value in enumerate((cross_re, cross_im, self_sq, left)):
-        part[0, i : i + 1, :] = jnp.broadcast_to(value, (1, LANES))
-
-    def scalar_copy(stage_, k):
-        return pltpu.make_async_remote_copy(
-            src_ref=part.at[stage_],
-            dst_ref=gath.at[stage_, (me, rad)[stage_]],
-            send_sem=sc_send.at[stage_, k],
-            recv_sem=sc_recv.at[stage_, k],
-            device_id=(chan_peer, rad_peer)[stage_](k),
-            device_id_type=MESH,
-        )
-
-    def merge(stage_):
-        for k in range(1, DEV):
-            scalar_copy(stage_, k).start()
-        gath[stage_, (me, rad)[stage_]] = part[stage_]
-        for k in range(1, DEV):
-            scalar_copy(stage_, k).wait_recv()
-        rows = [[gath[stage_, j, i : i + 1, :] for j in range(DEV)] for i in range(4)]
-        add = lambda xs: functools.reduce(lambda x, y: x + y, xs)
-        cre, cim, sq = add(rows[0]), add(rows[1]), add(rows[2])
-        pre, pim = ratio(cre, sq), ratio(cim, sq)
-        rest = add(rows[3])
-        for j in range(DEV):
-            dre = pre - ratio(rows[0][j], rows[2][j])
-            dim = pim - ratio(rows[1][j], rows[2][j])
-            rest = rest + (dre * dre + dim * dim) * rows[2][j]
-        return cre, cim, sq, rest, pre, pim
-
-    merged = merge(0)
-    for i in range(4):
-        part[1, i : i + 1, :] = merged[i]
-    _, _, _, rest, pre, pim = merge(1)
+    _, _, _, rest, pre, pim = take_all(1)
     rms = jnp.sqrt(rest / (2.0 * C * B * R) + 1e-06)
     place = lax.broadcasted_iota(jnp.int32, (1, 3), 1)
     coef_ref[...] = jnp.where(
         place == 0, pre[:, 0:3], jnp.where(place == 1, pim[:, 0:3], rms[:, 0:3])
     )
-    pre1, pim1 = pre[:, 0:1], pim[:, 0:1]
-    for q in range(Q):
-        for i in range(4):
-            re = slice(q * 64 + i * 8, q * 64 + i * 8 + 8)
-            im = slice(q * 64 + 32 + i * 8, q * 64 + 32 + i * 8 + 8)
-            sre, sim, are, aim = snat[re, :], snat[im, :], app[re, :], app[im, :]
-            ore = aim - (pre1 * sre - pim1 * sim)
-            oim = -are - (pre1 * sim + pim1 * sre)
-            for tile in range(R // LANES):
-                cols = slice(tile * LANES, tile * LANES + LANES)
-                rows = tile * 256 + 4 * q + i
-                rows_of[pl.ds(rows, 8, stride=2 * B), :] = ore[:, cols]
-                rows_of[pl.ds(rows + B, 8, stride=2 * B), :] = oim[:, cols]
     for tile in range(R // LANES):
-        out_ref[:, tile * LANES : tile * LANES + LANES] = rows_of[tile * 256 : tile * 256 + 256, :]
+        cols = slice(tile * LANES, tile * LANES + LANES)
+        for channel in range(8):
+            re = slice(tile * 256 + channel * 2 * B, tile * 256 + channel * 2 * B + B)
+            im = slice(re.stop, re.stop + B)
+            sre, sim, are, aim = s_nat[re, :], s_nat[im, :], a_nat[re, :], a_nat[im, :]
+            at = channel * 2 * B
+            out_ref[at : at + B, cols] = aim - (pre * sre - pim * sim)
+            out_ref[at + B : at + 2 * B, cols] = -are - (pre * sim + pim * sre)
 
     for k in range(1, DEV):
         live_copy(k).wait_send()
         state_copy(k).wait_send()
+        kinetic_copy(k).wait_send()
         scalar_copy(0, k).wait_send()
         scalar_copy(1, k).wait_send()
 
@@ -1356,9 +1408,12 @@
             pltpu.VMEM((Q, 128, CELLS), F32),
             pltpu.VMEM((DEV, Q, 8, CELLS), F32),
             pltpu.VMEM((Q, DEV, 8, CELLS), F32),
-            pltpu.VMEM((256, R), F32),
-            pltpu.VMEM((256, R), F32),
             pltpu.VMEM((R // LANES * 256, LANES), F32),
+            pltpu.VMEM((R // LANES * 256, LANES), F32),
+            pltpu.VMEM((R // LANES * 256, LANES), F32),
+            pltpu.VMEM((DEV, Q, 8, CELLS), F32),
+            pltpu.VMEM((Q, 128, CELLS), F32),
+            pltpu.VMEM((Q, 8, LANES), F32),
             pltpu.VMEM((2, 8, LANES), F32),
             pltpu.VMEM((2, DEV, 8, LANES), F32),
             pltpu.VMEM((8, LANES), jnp.int32),
@@ -1380,6 +1435,8 @@
             dma((DEV,)),
             dma((Q, DEV)),
             dma((Q, DEV)),
+            dma((DEV,)),
+            dma((DEV,)),
             dma((2, DEV)),
             dma((2, DEV)),
         ],

time: 133 us -> 125 us (0.940)
  Pallas kernels: 128 us -> 120 us
    pallas_call x1, Pallas kernels: 128 us -> 120 us  [per_device(): pl.pallas_call(kernel, out_shape=(jax.ShapeDtypeStruct((8 * 2 * B, R), F3...]
where the time goes in v3:
time: 125 us
  Pallas kernels  120 us (96%)
  local copies, waits for them, and re-layouts  3.22 us (3%)
  between operations  1.28 us (1%)
    pallas_call x1, Pallas kernels, per_device(): pl.pallas_call(kernel, out_shape=(jax.ShapeDtypeStruct((8 * 2 * B, R), F3...  120 us
    unnamed x10, local copies, waits for them, and re-layouts  3.22 us

profile of v3, /device:TPU:1, one launch (start us, length us, event | category | flops | bytes accessed | tf_op | source)
XLA Modules:
  0.0 124.6 jit_solution(14343038644404755209)
XLA Ops:
  0.6 0.0 copy-start
  0.6 0.0 copy-start.1
  0.6 0.0 copy-start.2
  0.7 119.9 %shard_map.95 = (f32[256,1536]{1,0:T(8,128)}, f32[1,3]{1,0:T(1,128)}, s32[1]{0:T(128)}) custom-call(f32[3072,128]{1,0:T(8,128)} %bitcast.14, f32[8192,32]{1,0:T(8,128)} %bitcast.11, s32[16,16]{1,0:T(8,128)} %fetch_ref.1, s32[4]{0:T(128)} %live_ref.1, f32[16]{0:T(128)} %r1_ref.1, f32[1,96]{1,0:T(1,128)} %bitcast.16, f32[12,128,128]{2,1,0:T(8,128)} %diag_hbm.1, ...), custom_call_target="tpu_custom_call" | custom-call | tf_op jit(solution)/shard_map/pallas_call | solution.py:1385
  121.1 0.0 copy-done
  121.1 0.0 copy-done.1
  121.1 0.0 copy-done.2
  121.1 0.3 conditional.1
  121.4 0.0 copy-start.3
  121.4 2.7 %copy.18 = f32[8,2,16,1536]{3,2,1,0:T(8,128)} copy(f32[8,2,16,1536]{3,2,1,0:T(8,128)} %bitcast.15) | data formatting | bytes 3145728
  124.1 0.0 copy-done.3
  124.1 0.5 copy.19
Async XLA Ops:
  0.6 120.5 %copy-start = (f32[128,2,16,96]{0,3,2,1:T(8,128)S(1)}, f32[128,2,16,96]{0,3,2,1:T(8,128)}, u32[]{:S(2)}) copy-start(f32[128,2,16,96]{0,3,2,1:T(8,128)} %param.10) | copy-start | bytes 4718596
  0.6 120.5 %copy-start.1 = (f32[12,128,128]{2,1,0:T(8,128)S(1)}, f32[12,128,128]{2,1,0:T(8,128)}, u32[]{:S(2)}) copy-start(f32[12,128,128]{2,1,0:T(8,128)} %diag_hbm.1) | copy-start | bytes 2359300
  0.6 120.5 %copy-start.2 = (f32[11,128,128]{2,1,0:T(8,128)S(1)}, f32[11,128,128]{2,1,0:T(8,128)}, u32[]{:S(2)}) copy-start(f32[11,128,128]{2,1,0:T(8,128)} %link_hbm.1) | copy-start | bytes 2162692
  121.4 2.7 %copy-start.3 = (f32[3]{0:T(128)S(1)}, f32[3]{0:T(128)}, u32[]{:S(2)}) copy-start(f32[3]{0:T(128)} %get-tuple-element.67) | copy-start | bytes 40
